TPU v7x, 32 devices: a whole 2x2x4 slice. The times are simulated.
32 devices in a mesh: dp: 8 (over y, x, core), tensor: 4 (over z).
Axes of the slice: x: 2, y: 2, z: 4, core: 2. Of those that a mesh axis runs over, the one named last changes fastest.
Arguments:
- tokens: bfloat16 [2, 16, 320, 1024], P(None, 'dp', 'tensor'), may hold values from -6 to 6
- cotangent: bfloat16 [2, 16, 320, 1024], P(None, 'dp', 'tensor'), may hold values from -6 to 6
- keep_mask: int32 [2, 16, 320], P(None, 'dp'), may hold values 0 or 1
- intake: float32 [3072, 1024], P(('tensor', 'dp')), may hold values from -0.1875 to 0.1875
- outlet: float32 [1024, 1024], P(('tensor', 'dp')), may hold values from -1.5 to 1.5
- expand: float32 [4096, 1024], P(('tensor', 'dp')), may hold values from -0.1875 to 0.1875
- shrink: float32 [4096, 1024], P(('tensor', 'dp')), may hold values from -0.09375 to 0.09375
- intake_moment: float32 [3072, 1024], P(('tensor', 'dp')), may hold values from -320 to 320
- outlet_moment: float32 [1024, 1024], P(('tensor', 'dp')), may hold values from -320 to 320
- expand_moment: float32 [4096, 1024], P(('tensor', 'dp')), may hold values from -320 to 320
- shrink_moment: float32 [4096, 1024], P(('tensor', 'dp')), may hold values from -320 to 320
- head_bias: float32 [2, 1024], replicated, may hold values from -1.75 to 1.75
- expand_bias: float32 [4096], replicated, may hold values from -1.75 to 1.75
- norm_gain: float32 [2, 1024], replicated, may hold values from 0.5 to 1.5
- model_bias: float32 [4, 1024], replicated, may hold values from -1.25 to 1.25
- head_first: float32 [2, 1024], replicated, may hold values from -256 to 256
- head_second: float32 [2, 1024], replicated, may hold values from 1000 to 30000
- expand_first: float32 [4096], replicated, may hold values from -32 to 32
- expand_second: float32 [4096], replicated, may hold values from 20 to 600
- gain_first: float32 [2, 1024], replicated, may hold values from -256 to 256
- gain_second: float32 [2, 1024], replicated, may hold values from 1000 to 30000
- bias_first: float32 [4, 1024], replicated, may hold values from -256 to 256
- bias_second: float32 [4, 1024], replicated, may hold values from 1000 to 30000
Outputs:
- output: float32 [2, 16, 320, 1024], P(None, 'dp', 'tensor')
- token_grad: float32 [2, 16, 320, 1024], P(None, 'dp', 'tensor')
- intake_grad: float32 [3072, 1024], P(('tensor', 'dp'))
- outlet_grad: float32 [1024, 1024], P(('tensor', 'dp'))
- expand_grad: float32 [4096, 1024], P(('tensor', 'dp'))
- shrink_grad: float32 [4096, 1024], P(('tensor', 'dp'))
- head_bias_grad: float32 [2, 1024], replicated
- expand_bias_grad: float32 [4096], replicated
- norm_gain_grad: float32 [2, 1024], replicated
- model_bias_grad: float32 [4, 1024], replicated
- intake_moment_new: float32 [3072, 1024], P(('tensor', 'dp'))
- outlet_moment_new: float32 [1024, 1024], P(('tensor', 'dp'))
- expand_moment_new: float32 [4096, 1024], P(('tensor', 'dp'))
- shrink_moment_new: float32 [4096, 1024], P(('tensor', 'dp'))
- intake_new: float32 [3072, 1024], P(('tensor', 'dp'))
- outlet_new: float32 [1024, 1024], P(('tensor', 'dp'))
- expand_new: float32 [4096, 1024], P(('tensor', 'dp'))
- shrink_new: float32 [4096, 1024], P(('tensor', 'dp'))
- intake_copy: bfloat16 [3072, 1024], P(('tensor', 'dp'))
- outlet_copy: bfloat16 [1024, 1024], P(('tensor', 'dp'))
- expand_copy: bfloat16 [4096, 1024], P(('tensor', 'dp'))
- shrink_copy: bfloat16 [4096, 1024], P(('tensor', 'dp'))
- head_bias_change: float32 [2, 1024], replicated
- expand_bias_change: float32 [4096], replicated
- norm_gain_change: float32 [2, 1024], replicated
- model_bias_change: float32 [4, 1024], replicated
- head_first_new: float32 [2, 1024], replicated
- head_second_new: float32 [2, 1024], replicated
- expand_first_new: float32 [4096], replicated
- expand_second_new: float32 [4096], replicated
- gain_first_new: float32 [2, 1024], replicated
- gain_second_new: float32 [2, 1024], replicated
- bias_first_new: float32 [4, 1024], replicated
- bias_second_new: float32 [4, 1024], replicated
All inputs are finite; a program needn't handle non-finite values. No bound on the sum of `keep_mask` on one device may be relied on, other than what follows from the above.
Results may differ from a plain program's by a relative error of at most 0.025.
Values may be sent and summed in bfloat16 or wider, within the bound.
A program may use at most 128 MiB of HBM per device.

v0:
```python
import jax
import jax.numpy as jnp
from jax import lax
from jax.sharding import PartitionSpec as P

HEAD_DIM = 64
BUF = 64
NS_STEPS = 5
ADAM_STEP = 10


norm_eps = 1e-06
first_decay = 0.9
second_decay = 0.95
adam_rate = 0.05
adam_eps = 1e-08
muon_decay = 0.5
muon_rates = (1.0, 4.0, 1.0, 1.0)
frob_eps = 1e-07
coef_a = 3.4445
coef_b = -4.775
coef_c = 2.0315
masked_score = -1000000000.0


def precise(form, left, right):
    return jnp.einsum(form, left, right, precision=lax.Precision.HIGHEST)


def layer_norm(inputs_row, gain_row, shift_row):
    center = inputs_row - jnp.mean(inputs_row, axis=-1, keepdims=True)
    spread = jnp.mean(center * center, axis=-1, keepdims=True)
    return center * lax.rsqrt(spread + norm_eps) * gain_row + shift_row


def softmax_rows(scores):
    largest = jnp.max(scores, axis=-1, keepdims=True)
    powers = jnp.exp(scores - largest)
    return powers / jnp.sum(powers, axis=-1, keepdims=True)


def exact_gelu(inputs_row):
    return jax.nn.gelu(inputs_row, approximate=False)


def attend_weights(queries, keys_all, live_keys):
    scores = jnp.einsum(
        "iqhe,ikhe->ihqk", queries, keys_all, preferred_element_type=jnp.float32
    ) * HEAD_DIM ** (-0.5)
    scores = jnp.where(live_keys[:, None, None, :], scores, masked_score)
    return softmax_rows(scores)


def reduce_blocks(blocks):
    return (
        lax.psum_scatter(blocks[0], "dp", scatter_dimension=0, tiled=True),
        lax.psum_scatter(blocks[1], "dp", scatter_dimension=0, tiled=True),
        lax.psum_scatter(blocks[2], "dp", scatter_dimension=0, tiled=True),
        lax.psum_scatter(blocks[3], "dp", scatter_dimension=0, tiled=True),
    )


def gram_whole(matrix):
    model_width = matrix.shape[1]
    own_rows = model_width // lax.axis_size("dp")
    shard_rows = lax.psum_scatter(
        precise(
            "rm,rn->mn", lax.slice_in_dim(matrix, 0, own_rows * lax.axis_size("dp"), axis=1), matrix
        ),
        "dp",
        scatter_dimension=0,
        tiled=True,
    )
    return lax.all_gather(shard_rows, "dp", axis=0, tiled=True)


def newton_step(scaled, gram):
    product = precise("rk,kn->rn", scaled, gram)
    return coef_a * scaled + coef_b * product + coef_c * precise("rk,kn->rn", product, gram)


def adam_step(gradient, first, second):
    first_new = first_decay * first + (1.0 - first_decay) * gradient
    second_new = second_decay * second + (1.0 - second_decay) * gradient * gradient
    first_hat = first_new / (1.0 - first_decay**ADAM_STEP)
    second_hat = second_new / (1.0 - second_decay**ADAM_STEP)
    change = -adam_rate * first_hat / (jnp.sqrt(second_hat) + adam_eps)
    return (change, first_new, second_new)


def per_device(
    tokens,
    cotangent,
    keep_mask,
    intake,
    outlet,
    expand,
    shrink,
    intake_moment,
    outlet_moment,
    expand_moment,
    shrink_moment,
    head_bias,
    expand_bias,
    norm_gain,
    model_bias,
    head_first,
    head_second,
    expand_first,
    expand_second,
    gain_first,
    gain_second,
    bias_first,
    bias_second,
):
    micro_count, images, local_seq, model_width = tokens.shape
    seq_len = keep_mask.shape[2]
    tensor_size = lax.axis_size("tensor")
    tensor_index = lax.axis_index("tensor")
    head_cols = model_width // tensor_size
    local_heads = head_cols // HEAD_DIM
    hidden_cols = expand_bias.shape[0] // tensor_size
    head_start = tensor_index * head_cols
    hidden_start = tensor_index * hidden_cols
    query_bias = lax.dynamic_slice_in_dim(head_bias[0], head_start, head_cols, 0).reshape(
        local_heads, HEAD_DIM
    )
    value_bias = lax.dynamic_slice_in_dim(head_bias[1], head_start, head_cols, 0).reshape(
        local_heads, HEAD_DIM
    )
    mixed_bias = jnp.stack([query_bias, jnp.zeros_like(query_bias), value_bias], axis=1).reshape(
        3 * head_cols
    )
    hidden_bias = lax.dynamic_slice_in_dim(expand_bias, hidden_start, hidden_cols, 0)
    position = jnp.arange(seq_len)
    masters = (intake, outlet, expand, shrink)
    block_shapes = (
        (3 * head_cols, model_width),
        (head_cols, model_width),
        (hidden_cols, model_width),
        (hidden_cols, model_width),
    )
    totals = tuple((jnp.zeros(shape_one, jnp.float32) for shape_one in block_shapes))
    gain_grad = jnp.zeros((2, model_width), jnp.float32)
    bias_grad = jnp.zeros((4, model_width), jnp.float32)
    mixed_bias_grad = jnp.zeros((2, head_cols), jnp.float32)
    hidden_bias_grad = jnp.zeros((hidden_cols,), jnp.float32)
    outputs = []
    token_grads = []
    for micro_index in range(micro_count):
        intake_block, outlet_block, expand_block, shrink_block = (
            lax.all_gather(intake.astype(jnp.bfloat16), "dp", axis=0, tiled=True),
            lax.all_gather(outlet.astype(jnp.bfloat16), "dp", axis=0, tiled=True),
            lax.all_gather(expand.astype(jnp.bfloat16), "dp", axis=0, tiled=True),
            lax.all_gather(shrink.astype(jnp.bfloat16), "dp", axis=0, tiled=True),
        )
        token_rows = tokens[micro_index].astype(jnp.float32)
        live_keys = jnp.logical_or(keep_mask[micro_index] > 0, position[None, :] < BUF)
        first_local = layer_norm(token_rows, norm_gain[0], model_bias[0]).astype(jnp.bfloat16)
        first_norm = lax.all_gather(first_local, "tensor", axis=1, tiled=True)
        mixed_rows = (
            jnp.einsum("isd,rd->isr", first_norm, intake_block, preferred_element_type=jnp.float32)
            + mixed_bias
        )
        mixed_rows = mixed_rows.astype(jnp.bfloat16).reshape(
            images, seq_len, local_heads, 3, HEAD_DIM
        )
        queries = mixed_rows[:, :, :, 0]
        keys_all = mixed_rows[:, :, :, 1]
        values = mixed_rows[:, :, :, 2]
        attention = attend_weights(queries, keys_all, live_keys)
        attention_low = attention.astype(jnp.bfloat16)
        attended = jnp.einsum(
            "ihqk,ikhe->iqhe", attention_low, values, preferred_element_type=jnp.float32
        )
        attended = attended.reshape(images, seq_len, head_cols).astype(jnp.bfloat16)
        part_sum = jnp.einsum(
            "isc,cd->isd", attended, outlet_block, preferred_element_type=jnp.float32
        )
        middle = (
            token_rows
            + lax.psum_scatter(part_sum, "tensor", scatter_dimension=1, tiled=True)
            + model_bias[2]
        )
        second_local = layer_norm(middle, norm_gain[1], model_bias[1]).astype(jnp.bfloat16)
        second_norm = lax.all_gather(second_local, "tensor", axis=1, tiled=True)
        hidden = (
            jnp.einsum("isd,fd->isf", second_norm, expand_block, preferred_element_type=jnp.float32)
            + hidden_bias
        )
        active = exact_gelu(hidden).astype(jnp.bfloat16)
        part_two = jnp.einsum(
            "isf,fd->isd", active, shrink_block, preferred_element_type=jnp.float32
        )
        outputs.append(
            middle
            + lax.psum_scatter(part_two, "tensor", scatter_dimension=1, tiled=True)
            + model_bias[3]
        )
        cot_local = cotangent[micro_index]
        cot_rows = lax.all_gather(cot_local, "tensor", axis=1, tiled=True)
        shrink_block_grad = jnp.einsum(
            "isf,isd->fd", active, cot_rows, preferred_element_type=jnp.float32
        )
        active_grad = jnp.einsum(
            "isd,fd->isf", cot_rows, shrink_block, preferred_element_type=jnp.float32
        )
        gelu_value, gelu_back = jax.vjp(exact_gelu, hidden)
        hidden_grad = gelu_back(active_grad)[0].astype(jnp.bfloat16)
        hidden_bias_grad = hidden_bias_grad + jnp.sum(hidden_grad.astype(jnp.float32), axis=(0, 1))
        expand_block_grad = jnp.einsum(
            "isf,isd->fd", hidden_grad, second_norm, preferred_element_type=jnp.float32
        )
        second_part = jnp.einsum(
            "isf,fd->isd", hidden_grad, expand_block, preferred_element_type=jnp.float32
        )
        second_grad = lax.psum_scatter(second_part, "tensor", scatter_dimension=1, tiled=True)
        norm_value, norm_back = jax.vjp(layer_norm, middle, norm_gain[1], model_bias[1])
        middle_from_norm, gain_two_grad, shift_two_grad = norm_back(second_grad)
        cot_float = cot_local.astype(jnp.float32)
        middle_grad = cot_float + middle_from_norm
        branch_grad = middle_grad.astype(jnp.bfloat16)
        branch_rows = lax.all_gather(branch_grad, "tensor", axis=1, tiled=True)
        outlet_block_grad = jnp.einsum(
            "isc,isd->cd", attended, branch_rows, preferred_element_type=jnp.float32
        )
        attended_grad = jnp.einsum(
            "isd,cd->isc", branch_rows, outlet_block, preferred_element_type=jnp.float32
        )
        attended_grad = attended_grad.astype(jnp.bfloat16).reshape(
            images, seq_len, local_heads, HEAD_DIM
        )
        attention = attend_weights(queries, keys_all, live_keys)
        attention_low = attention.astype(jnp.bfloat16)
        values_grad = jnp.einsum(
            "ihqk,iqhe->ikhe", attention_low, attended_grad, preferred_element_type=jnp.float32
        )
        attention_grad = jnp.einsum(
            "iqhe,ikhe->ihqk", attended_grad, values, preferred_element_type=jnp.float32
        )
        score_grad = attention * (
            attention_grad - jnp.sum(attention_grad * attention, axis=-1, keepdims=True)
        )
        score_grad = score_grad.astype(jnp.bfloat16)
        queries_grad = jnp.einsum(
            "ihqk,ikhe->iqhe", score_grad, keys_all, preferred_element_type=jnp.float32
        ) * HEAD_DIM ** (-0.5)
        keys_grad = jnp.einsum(
            "ihqk,iqhe->ikhe", score_grad, queries, preferred_element_type=jnp.float32
        ) * HEAD_DIM ** (-0.5)
        mixed_grad = jnp.stack([queries_grad, keys_grad, values_grad], axis=3).astype(jnp.bfloat16)
        mixed_sums = jnp.sum(mixed_grad.astype(jnp.float32), axis=(0, 1))
        mixed_bias_grad = mixed_bias_grad + jnp.stack(
            [mixed_sums[:, 0].reshape(head_cols), mixed_sums[:, 2].reshape(head_cols)]
        )
        mixed_grad = mixed_grad.reshape(images, seq_len, 3 * head_cols)
        intake_block_grad = jnp.einsum(
            "isr,isd->rd", mixed_grad, first_norm, preferred_element_type=jnp.float32
        )
        first_part = jnp.einsum(
            "isr,rd->isd", mixed_grad, intake_block, preferred_element_type=jnp.float32
        )
        first_grad = lax.psum_scatter(first_part, "tensor", scatter_dimension=1, tiled=True)
        first_value, first_back = jax.vjp(layer_norm, token_rows, norm_gain[0], model_bias[0])
        token_from_norm, gain_one_grad, shift_one_grad = first_back(first_grad)
        token_grads.append(middle_grad + token_from_norm)
        gain_grad = gain_grad + jnp.stack([gain_one_grad, gain_two_grad])
        bias_grad = bias_grad + jnp.stack(
            [
                shift_one_grad,
                shift_two_grad,
                jnp.sum(branch_grad.astype(jnp.float32), axis=(0, 1)),
                jnp.sum(cot_float, axis=(0, 1)),
            ]
        )
        block_grads = (intake_block_grad, outlet_block_grad, expand_block_grad, shrink_block_grad)
        totals = tuple((total + block_one for total, block_one in zip(totals, block_grads)))
    shards = reduce_blocks(totals)
    head_full = lax.dynamic_update_slice_in_dim(
        jnp.zeros((2, model_width), jnp.float32), mixed_bias_grad, head_start, 1
    )
    hidden_full = lax.dynamic_update_slice_in_dim(
        jnp.zeros(expand_bias.shape, jnp.float32), hidden_bias_grad, hidden_start, 0
    )
    gain_total, bias_total, head_total, hidden_total = lax.psum(
        (gain_grad, bias_grad, head_full, hidden_full), ("dp", "tensor")
    )
    moments = (intake_moment, outlet_moment, expand_moment, shrink_moment)
    moments_new = [muon_decay * moment + gradient for gradient, moment in zip(shards, moments)]
    updates = [gradient + muon_decay * moment for gradient, moment in zip(shards, moments_new)]
    rows_max = max((update.shape[0] for update in updates))
    padded = jnp.stack(
        [jnp.pad(update, ((0, rows_max - update.shape[0]), (0, 0))) for update in updates]
    )
    spread = lax.all_to_all(padded, "tensor", split_axis=0, concat_axis=0, tiled=True)
    own_matrix = spread.reshape(tensor_size * rows_max, model_width)
    raw_gram = gram_whole(own_matrix)
    measure = jnp.sqrt(jnp.trace(raw_gram)) + frob_eps
    scaled = own_matrix / measure
    gram = raw_gram / (measure * measure)
    for step in range(NS_STEPS):
        if step > 0:
            gram = gram_whole(scaled)
        scaled = newton_step(scaled, gram)
    returned = lax.all_to_all(
        scaled.reshape(tensor_size, rows_max, model_width),
        "tensor",
        split_axis=0,
        concat_axis=0,
        tiled=True,
    )
    rows_scale = lax.axis_size("dp") * tensor_size
    masters_new = [
        weight
        - muon_rates[position_one]
        * (weight.shape[0] * rows_scale / weight.shape[1]) ** 0.5
        * returned[position_one, : weight.shape[0]]
        for position_one, weight in enumerate(masters)
    ]
    head_bias_change, head_first_new, head_second_new = adam_step(
        head_total, head_first, head_second
    )
    expand_bias_change, expand_first_new, expand_second_new = adam_step(
        hidden_total, expand_first, expand_second
    )
    norm_gain_change, gain_first_new, gain_second_new = adam_step(
        gain_total, gain_first, gain_second
    )
    model_bias_change, bias_first_new, bias_second_new = adam_step(
        bias_total, bias_first, bias_second
    )
    output = jnp.stack(outputs)
    token_grad = jnp.stack(token_grads)
    return (
        output,
        token_grad,
        shards[0],
        shards[1],
        shards[2],
        shards[3],
        head_total,
        hidden_total,
        gain_total,
        bias_total,
        moments_new[0],
        moments_new[1],
        moments_new[2],
        moments_new[3],
        masters_new[0],
        masters_new[1],
        masters_new[2],
        masters_new[3],
        masters_new[0].astype(jnp.bfloat16),
        masters_new[1].astype(jnp.bfloat16),
        masters_new[2].astype(jnp.bfloat16),
        masters_new[3].astype(jnp.bfloat16),
        head_bias_change,
        expand_bias_change,
        norm_gain_change,
        model_bias_change,
        head_first_new,
        head_second_new,
        expand_first_new,
        expand_second_new,
        gain_first_new,
        gain_second_new,
        bias_first_new,
        bias_second_new,
    )


def solution(mesh):
    placed = (
        P(None, "dp", "tensor", None),
        P(None, "dp", "tensor", None),
        P(None, "dp", None),
        P(("tensor", "dp"), None),
        P(("tensor", "dp"), None),
        P(("tensor", "dp"), None),
        P(("tensor", "dp"), None),
        P(("tensor", "dp"), None),
        P(("tensor", "dp"), None),
        P(("tensor", "dp"), None),
        P(("tensor", "dp"), None),
        P(),
        P(),
        P(),
        P(),
        P(),
        P(),
        P(),
        P(),
        P(),
        P(),
        P(),
        P(),
    )
    return jax.shard_map(
        per_device,
        mesh=mesh,
        in_specs=placed,
        out_specs=(
            P(None, "dp", "tensor", None),
            P(None, "dp", "tensor", None),
            P(("tensor", "dp"), None),
            P(("tensor", "dp"), None),
            P(("tensor", "dp"), None),
            P(("tensor", "dp"), None),
            P(),
            P(),
            P(),
            P(),
            P(("tensor", "dp"), None),
            P(("tensor", "dp"), None),
            P(("tensor", "dp"), None),
            P(("tensor", "dp"), None),
            P(("tensor", "dp"), None),
            P(("tensor", "dp"), None),
            P(("tensor", "dp"), None),
            P(("tensor", "dp"), None),
            P(("tensor", "dp"), None),
            P(("tensor", "dp"), None),
            P(("tensor", "dp"), None),
            P(("tensor", "dp"), None),
            P(),
            P(),
            P(),
            P(),
            P(),
            P(),
            P(),
            P(),
            P(),
            P(),
            P(),
            P(),
        ),
        check_vma=False,
    )
```

profile of v0, /device:TPU:8, one launch (start us, length us, event | category | flops | bytes accessed | tf_op | source)
XLA Modules:
  0.0 1725.7 jit_solution(14054624792649160089)
XLA Ops:
  16.1 9.9 all_gather.57
  26.0 21.4 %all-gather.29.cloned.1.call-done = bf16[2,320,1024]{2,1,0:T(8,128)(2,1)} async-done(((bf16[2,80,1024]{2,1,0:T(8,128)(2,1)}), bf16[2,320,1024]{2,1,0:T(8,128)(2,1)}) %all-gather.29.cloned.1.call-update) | async-done | bytes 1310736 | tf_op jit(solution)/shard_map/all_gather | solution.py:160
  47.4 27.9 %all-gather.21.cloned.1.call-done = bf16[768,1024]{1,0:T(8,128)(2,1)} async-done(((bf16[96,1024]{1,0:T(8,128)(2,1)}), bf16[768,1024]{1,0:T(8,128)(2,1)}) %all-gather.21.cloned.1.call-update) | async-done | bytes 1572880 | tf_op jit(solution)/shard_map/all_gather | solution.py:152
  88.1 21.3 %all-gather.19.cloned.1.call-done = bf16[2,320,1024]{2,1,0:T(8,128)(2,1)} async-done(((bf16[2,80,1024]{2,1,0:T(8,128)(2,1)}), bf16[2,320,1024]{2,1,0:T(8,128)(2,1)}) %all-gather.19.cloned.1.call-update) | async-done | bytes 1310736 | tf_op jit(solution)/shard_map/all_gather | solution.py:160
  123.4 39.2 %reduce-scatter.22.cloned.1.call-done = f32[2,80,1024]{2,1,0:T(8,128)} async-done(((f32[2,320,1024]{2,1,0:T(8,128)}), f32[2,80,1024]{2,1,0:T(8,128)}) %reduce-scatter.22.cloned.1.call-update) | async-done | bytes 655376 | tf_op jit(solution)/shard_map/reduce_scatter | solution.py:182
  162.6 54.0 %reduce-scatter.18.cloned.1.call-done = f32[2,80,1024]{2,1,0:T(8,128)} async-done(((f32[2,320,1024]{2,1,0:T(8,128)}), f32[2,80,1024]{2,1,0:T(8,128)}) %reduce-scatter.18.cloned.1.call-update) | async-done | bytes 655376 | tf_op jit(solution)/shard_map/reduce_scatter | solution.py:182
  224.0 23.3 %all-gather.25.cloned.1.call-done = bf16[1024,1024]{1,0:T(8,128)(2,1)} async-done(((bf16[128,1024]{1,0:T(8,128)(2,1)}), bf16[1024,1024]{1,0:T(8,128)(2,1)}) %all-gather.25.cloned.1.call-update) | async-done | bytes 2097168 | tf_op jit(solution)/shard_map/all_gather | solution.py:154
  247.4 34.2 %all-gather.31.cloned.1.call-done = bf16[2,320,1024]{2,1,0:T(8,128)(2,1)} async-done(((bf16[2,80,1024]{2,1,0:T(8,128)(2,1)}), bf16[2,320,1024]{2,1,0:T(8,128)(2,1)}) %all-gather.31.cloned.1.call-update) | async-done | bytes 1310736 | tf_op jit(solution)/shard_map/all_gather | solution.py:186
  286.5 28.8 %all-gather.23.cloned.1.call-done = bf16[2,320,1024]{2,1,0:T(8,128)(2,1)} async-done(((bf16[2,80,1024]{2,1,0:T(8,128)(2,1)}), bf16[2,320,1024]{2,1,0:T(8,128)(2,1)}) %all-gather.23.cloned.1.call-update) | async-done | bytes 1310736 | tf_op jit(solution)/shard_map/all_gather | solution.py:186
  323.1 13.5 multiply_convert_fusion.3
  336.6 12.6 all-gather.49.cloned.1.call-done
  349.3 29.9 %all-gather.27.cloned.1.call-done = bf16[1024,1024]{1,0:T(8,128)(2,1)} async-done(((bf16[128,1024]{1,0:T(8,128)(2,1)}), bf16[1024,1024]{1,0:T(8,128)(2,1)}) %all-gather.27.cloned.1.call-update) | async-done | bytes 2097168 | tf_op jit(solution)/shard_map/all_gather | solution.py:155
  390.4 22.9 %all-gather.47.cloned.1.call-done = bf16[1,2,320,1024]{3,2,1,0:T(8,128)(2,1)} async-done(((bf16[1,2,80,1024]{3,2,1,0:T(8,128)(2,1)}), bf16[1,2,320,1024]{3,2,1,0:T(8,128)(2,1)}) %all-gather.47.cloned.1.call-update) | async-done | bytes 1310736 | tf_op jit(solution)/shard_map/all_gather | solution.py:201
  434.5 32.1 %reduce-scatter.30.cloned.1.call-done = f32[2,80,1024]{2,1,0:T(8,128)} async-done(((f32[2,320,1024]{2,1,0:T(8,128)}), f32[2,80,1024]{2,1,0:T(8,128)}) %reduce-scatter.30.cloned.1.call-update) | async-done | bytes 655376 | tf_op jit(solution)/shard_map/reduce_scatter | solution.py:217
  466.6 54.1 %reduce-scatter.26.cloned.1.call-done = f32[2,80,1024]{2,1,0:T(8,128)} async-done(((f32[2,320,1024]{2,1,0:T(8,128)}), f32[2,80,1024]{2,1,0:T(8,128)}) %reduce-scatter.26.cloned.1.call-update) | async-done | bytes 655376 | tf_op jit(solution)/shard_map/reduce_scatter | solution.py:217
  523.1 51.6 %reduce-scatter.20.cloned.1.call-done = f32[2,80,1024]{2,1,0:T(8,128)} async-done(((f32[2,320,1024]{2,1,0:T(8,128)}), f32[2,80,1024]{2,1,0:T(8,128)}) %reduce-scatter.20.cloned.1.call-update) | async-done | bytes 655376 | tf_op jit(solution)/shard_map/reduce_scatter | solution.py:197
  574.6 54.0 %reduce-scatter.24.cloned.1.call-done = f32[2,80,1024]{2,1,0:T(8,128)} async-done(((f32[2,320,1024]{2,1,0:T(8,128)}), f32[2,80,1024]{2,1,0:T(8,128)}) %reduce-scatter.24.cloned.1.call-update) | async-done | bytes 655376 | tf_op jit(solution)/shard_map/reduce_scatter | solution.py:197
  650.7 16.2 all-gather.35.cloned.1.call-done
  669.6 30.9 %all-gather.33.cloned.1.call-done = bf16[2,320,1024]{2,1,0:T(8,128)(2,1)} async-done(((bf16[2,80,1024]{2,1,0:T(8,128)(2,1)}), bf16[2,320,1024]{2,1,0:T(8,128)(2,1)}) %all-gather.33.cloned.1.call-update) | async-done | bytes 1310736 | tf_op jit(solution)/shard_map/all_gather | solution.py:223
  731.2 24.3 %reduce-scatter.38.cloned.1.call-done = f32[128,1024]{1,0:T(8,128)} async-done(((f32[1024,1024]{1,0:T(8,128)}), f32[128,1024]{1,0:T(8,128)}) %reduce-scatter.38.cloned.1.call-update) | async-done | bytes 524304 | tf_op jit(solution)/shard_map/reduce_scatter | solution.py:58
  757.4 53.7 %reduce-scatter.40.cloned.1.call-done = f32[128,1024]{1,0:T(8,128)} async-done(((f32[1024,1024]{1,0:T(8,128)}), f32[128,1024]{1,0:T(8,128)}) %reduce-scatter.40.cloned.1.call-update) | async-done | bytes 524304 | tf_op jit(solution)/shard_map/reduce_scatter | solution.py:59
  813.1 37.7 %reduce-scatter.36.cloned.1.call-done = f32[32,1024]{1,0:T(8,128)} async-done(((f32[256,1024]{1,0:T(8,128)}), f32[32,1024]{1,0:T(8,128)}) %reduce-scatter.36.cloned.1.call-update) | async-done | bytes 131088 | tf_op jit(solution)/shard_map/reduce_scatter | solution.py:57
  852.4 48.6 %reduce-scatter.34.cloned.1.call-done = f32[96,1024]{1,0:T(8,128)} async-done(((f32[768,1024]{1,0:T(8,128)}), f32[96,1024]{1,0:T(8,128)}) %reduce-scatter.34.cloned.1.call-update) | async-done | bytes 393232 | tf_op jit(solution)/shard_map/reduce_scatter | solution.py:56
  903.1 51.3 %all_to_all.10 = f32[4,128,1024]{2,1,0:T(8,128)S(1)} all-to-all(f32[4,128,1024]{2,1,0:T(8,128)S(1)} %pad_maximum_fusion), channel_id=1, replica_groups=mesh['dp'=8,'tensor'=4] {'tensor'}, dimensions={0} | all-to-all | bytes 4194304 | tf_op jit(solution)/shard_map/all_to_all | solution.py:295
  954.4 8.3 convolution_bitcast_fusion
  962.8 51.0 %reduce-scatter.42.cloned.1.call-done = f32[128,1024]{1,0:T(8,128)} async-done(((f32[1024,1024]{1,0:T(8,128)}), f32[128,1024]{1,0:T(8,128)}) %reduce-scatter.42.cloned.1.call-update) | async-done | bytes 524304 | tf_op jit(solution)/shard_map/reduce_scatter | solution.py:66
  1014.3 38.1 %all-gather.37.cloned.1.call-done = f32[1024,1024]{1,0:T(8,128)} async-done(((f32[128,1024]{1,0:T(8,128)}), f32[1024,1024]{1,0:T(8,128)}) %all-gather.37.cloned.1.call-update) | async-done | bytes 4194320 | tf_op jit(solution)/shard_map/all_gather | solution.py:74
  1072.3 8.5 fusion.175
  1080.8 51.5 %reduce-scatter.44.cloned.1.call-done = f32[128,1024]{1,0:T(8,128)} async-done(((f32[1024,1024]{1,0:T(8,128)}), f32[128,1024]{1,0:T(8,128)}) %reduce-scatter.44.cloned.1.call-update) | async-done | bytes 524304 | tf_op jit(solution)/shard_map/reduce_scatter | solution.py:66
  1132.4 38.7 %all-gather.39.cloned.1.call-done = f32[1024,1024]{1,0:T(8,128)} async-done(((f32[128,1024]{1,0:T(8,128)}), f32[1024,1024]{1,0:T(8,128)}) %all-gather.39.cloned.1.call-update) | async-done | bytes 4194320 | tf_op jit(solution)/shard_map/all_gather | solution.py:74
  1171.1 9.1 fusion.176
  1180.2 8.7 multiply_add_fusion.3
  1189.0 8.7 fusion.177
  1197.8 51.4 %reduce-scatter.46.cloned.1.call-done = f32[128,1024]{1,0:T(8,128)} async-done(((f32[1024,1024]{1,0:T(8,128)}), f32[128,1024]{1,0:T(8,128)}) %reduce-scatter.46.cloned.1.call-update) | async-done | bytes 524304 | tf_op jit(solution)/shard_map/reduce_scatter | solution.py:66
  1249.3 38.4 %all-gather.41.cloned.1.call-done = f32[1024,1024]{1,0:T(8,128)} async-done(((f32[128,1024]{1,0:T(8,128)}), f32[1024,1024]{1,0:T(8,128)}) %all-gather.41.cloned.1.call-update) | async-done | bytes 4194320 | tf_op jit(solution)/shard_map/all_gather | solution.py:74
  1287.7 9.1 fusion.178
  1305.3 8.5 fusion.179
  1313.9 51.5 %reduce-scatter.48.cloned.1.call-done = f32[128,1024]{1,0:T(8,128)} async-done(((f32[1024,1024]{1,0:T(8,128)}), f32[128,1024]{1,0:T(8,128)}) %reduce-scatter.48.cloned.1.call-update) | async-done | bytes 524304 | tf_op jit(solution)/shard_map/reduce_scatter | solution.py:66
  1365.4 38.7 %all-gather.43.cloned.1.call-done = f32[1024,1024]{1,0:T(8,128)} async-done(((f32[128,1024]{1,0:T(8,128)}), f32[1024,1024]{1,0:T(8,128)}) %all-gather.43.cloned.1.call-update) | async-done | bytes 4194320 | tf_op jit(solution)/shard_map/all_gather | solution.py:74
  1404.1 9.1 fusion.180
  1420.4 8.3 fusion.181
  1428.8 51.4 %reduce-scatter.50.cloned.1.call-done = f32[128,1024]{1,0:T(8,128)} async-done(((f32[1024,1024]{1,0:T(8,128)}), f32[128,1024]{1,0:T(8,128)}) %reduce-scatter.50.cloned.1.call-update) | async-done | bytes 524304 | tf_op jit(solution)/shard_map/reduce_scatter | solution.py:66
  1492.8 26.1 %all-gather.45.cloned.1.call-done = f32[1024,1024]{1,0:T(8,128)} async-done(((f32[128,1024]{1,0:T(8,128)}), f32[1024,1024]{1,0:T(8,128)}) %all-gather.45.cloned.1.call-update) | async-done | bytes 4194320 | tf_op jit(solution)/shard_map/all_gather | solution.py:74
  1518.9 9.3 fusion.182
  1528.3 8.5 multiply_add_fusion
  1542.5 65.6 %reduce-scatter.32.cloned.1.call-done = f32[2,80,1024]{2,1,0:T(8,128)} async-done(((f32[2,320,1024]{2,1,0:T(8,128)}), f32[2,80,1024]{2,1,0:T(8,128)}) %reduce-scatter.32.cloned.1.call-update) | async-done | bytes 655376 | tf_op jit(solution)/shard_map/reduce_scatter | solution.py:263
  1608.1 54.4 %reduce-scatter.28.cloned.1.call-done = f32[2,80,1024]{2,1,0:T(8,128)} async-done(((f32[2,320,1024]{2,1,0:T(8,128)}), f32[2,80,1024]{2,1,0:T(8,128)}) %reduce-scatter.28.cloned.1.call-update) | async-done | bytes 655376 | tf_op jit(solution)/shard_map/reduce_scatter | solution.py:263
  1666.3 40.6 %all-reduce.2 = (f32[2,1024]{1,0:T(2,128)S(1)}, f32[4096]{0:T(1024)S(1)}, f32[2,1024]{1,0:T(2,128)S(1)}, f32[4,1024]{1,0:T(4,128)S(1)}) all-reduce(f32[2,1024]{1,0:T(2,128)S(1)} %fusion.134, f32[4096]{0:T(1024)S(1)} %add_dynamic-update-slice_fusion, ...), channel_id=1, replica_groups=mesh['dp'=8,'tensor'=4] {'dp','tensor'}, use_global_device_ids=true, to_apply=%region_36.37 | all-reduce | flops 12288 | bytes 98304 | tf_op jit(solution)/shard_map/psum | solution.py:285
  (396 shorter events, 221.5 us)
Async XLA Ops:
  7.3 40.1 %all-gather.29.cloned.1.call-start = ((), (), s32[]{:S(2)}) async-start(), calls=%async_computation.26 | async-start | bytes 1638400 | tf_op jit(solution)/shard_map/all_gather | solution.py:160
  14.1 61.2 %all-gather.21.cloned.1.call-start = ((), (), s32[]{:S(2)}) async-start(), calls=%async_computation.20 | async-start | bytes 1769472 | tf_op jit(solution)/shard_map/all_gather | solution.py:152
  14.8 94.6 %all-gather.19.cloned.1.call-start = ((), (), s32[]{:S(2)}) async-start(), calls=%async_computation.19 | async-start | bytes 1638400 | tf_op jit(solution)/shard_map/all_gather | solution.py:160
  15.6 147.0 %reduce-scatter.22.cloned.1.call-start = ((), (), s32[]{:S(2)}) async-start(), calls=%async_computation.27 | async-start | bytes 3276800 | tf_op jit(solution)/shard_map/reduce_scatter | solution.py:182
  88.0 128.5 %reduce-scatter.18.cloned.1.call-start = ((), (), s32[]{:S(2)}) async-start(), calls=%async_computation.21 | async-start | bytes 3276800 | tf_op jit(solution)/shard_map/reduce_scatter | solution.py:182
  122.5 124.8 %all-gather.25.cloned.1.call-start = ((), (), s32[]{:S(2)}) async-start(), calls=%async_computation.23 | async-start | bytes 2359296 | tf_op jit(solution)/shard_map/all_gather | solution.py:154
  123.4 158.2 %all-gather.31.cloned.1.call-start = ((), (), s32[]{:S(2)}) async-start(), calls=%async_computation.28 | async-start | bytes 1638400 | tf_op jit(solution)/shard_map/all_gather | solution.py:186
  219.8 95.6 %all-gather.23.cloned.1.call-start = ((), (), s32[]{:S(2)}) async-start(), calls=%async_computation.22 | async-start | bytes 1638400 | tf_op jit(solution)/shard_map/all_gather | solution.py:186
  220.5 128.7 %all-gather.49.cloned.1.call-start = ((), (), s32[]{:S(2)}) async-start(), calls=%async_computation.51 | async-start | bytes 1638400 | tf_op jit(solution)/shard_map/all_gather | solution.py:201
  221.5 157.7 %all-gather.27.cloned.1.call-start = ((), (), s32[]{:S(2)}) async-start(), calls=%async_computation.24 | async-start | bytes 2359296 | tf_op jit(solution)/shard_map/all_gather | solution.py:155
  222.3 191.0 %all-gather.47.cloned.1.call-start = ((), (), s32[]{:S(2)}) async-start(), calls=%async_computation.50 | async-start | bytes 1638400 | tf_op jit(solution)/shard_map/all_gather | solution.py:201
  223.1 243.5 %reduce-scatter.30.cloned.1.call-start = ((), (), s32[]{:S(2)}) async-start(), calls=%async_computation.33 | async-start | bytes 3276800 | tf_op jit(solution)/shard_map/reduce_scatter | solution.py:217
  390.0 130.7 %reduce-scatter.26.cloned.1.call-start = ((), (), s32[]{:S(2)}) async-start(), calls=%async_computation.30 | async-start | bytes 3276800 | tf_op jit(solution)/shard_map/reduce_scatter | solution.py:217
  424.2 150.5 %reduce-scatter.20.cloned.1.call-start = ((), (), s32[]{:S(2)}) async-start(), calls=%async_computation.25 | async-start | bytes 3276800 | tf_op jit(solution)/shard_map/reduce_scatter | solution.py:197
  429.3 199.3 %reduce-scatter.24.cloned.1.call-start = ((), (), s32[]{:S(2)}) async-start(), calls=%async_computation.29 | async-start | bytes 3276800 | tf_op jit(solution)/shard_map/reduce_scatter | solution.py:197
  434.4 232.5 %all-gather.35.cloned.1.call-start = ((), (), s32[]{:S(2)}) async-start(), calls=%async_computation.34 | async-start | bytes 1638400 | tf_op jit(solution)/shard_map/all_gather | solution.py:223
  466.5 162.1 %copy-start.24 = (f32[2,80,1024]{2,1,0:T(8,128)S(1)}, f32[2,80,1024]{2,1,0:T(8,128)}, u32[]{:S(2)}) copy-start(f32[2,80,1024]{2,1,0:T(8,128)} %reduce-scatter.30.cloned.1.call-done) | copy-start | bytes 1966084
  634.2 66.4 %all-gather.33.cloned.1.call-start = ((), (), s32[]{:S(2)}) async-start(), calls=%async_computation.31 | async-start | bytes 1638400 | tf_op jit(solution)/shard_map/all_gather | solution.py:223
  634.8 120.7 %reduce-scatter.38.cloned.1.call-start = ((), (), s32[]{:S(2)}) async-start(), calls=%async_computation.38 | async-start | bytes 4718592 | tf_op jit(solution)/shard_map/reduce_scatter | solution.py:58
  642.6 168.5 %reduce-scatter.40.cloned.1.call-start = ((), (), s32[]{:S(2)}) async-start(), calls=%async_computation.39 | async-start | bytes 4718592 | tf_op jit(solution)/shard_map/reduce_scatter | solution.py:59
  650.6 200.2 %reduce-scatter.36.cloned.1.call-start = ((), (), s32[]{:S(2)}) async-start(), calls=%async_computation.37 | async-start | bytes 1179648 | tf_op jit(solution)/shard_map/reduce_scatter | solution.py:57
  721.9 179.1 %reduce-scatter.34.cloned.1.call-start = ((), (), s32[]{:S(2)}) async-start(), calls=%async_computation.36 | async-start | bytes 3538944 | tf_op jit(solution)/shard_map/reduce_scatter | solution.py:56
  731.1 169.9 %copy-start.46 = (f32[96,1024]{1,0:T(8,128)S(1)}, f32[96,1024]{1,0:T(8,128)}, u32[]{:S(2)}) copy-start(f32[96,1024]{1,0:T(8,128)} %param.30) | copy-start | bytes 1179652
  731.1 282.7 %reduce-scatter.42.cloned.1.call-start = ((), (), s32[]{:S(2)}) async-start(), calls=%async_computation.40 | async-start | bytes 4718592 | tf_op jit(solution)/shard_map/reduce_scatter | solution.py:66
  962.8 89.7 %all-gather.37.cloned.1.call-start = ((), (), s32[]{:S(2)}) async-start(), calls=%async_computation.41 | async-start | bytes 4718592 | tf_op jit(solution)/shard_map/all_gather | solution.py:74
  1013.8 118.5 %reduce-scatter.44.cloned.1.call-start = ((), (), s32[]{:S(2)}) async-start(), calls=%async_computation.42 | async-start | bytes 4718592 | tf_op jit(solution)/shard_map/reduce_scatter | solution.py:66
  1080.8 90.3 %all-gather.39.cloned.1.call-start = ((), (), s32[]{:S(2)}) async-start(), calls=%async_computation.43 | async-start | bytes 4718592 | tf_op jit(solution)/shard_map/all_gather | solution.py:74
  1132.3 116.9 %reduce-scatter.46.cloned.1.call-start = ((), (), s32[]{:S(2)}) async-start(), calls=%async_computation.44 | async-start | bytes 4718592 | tf_op jit(solution)/shard_map/reduce_scatter | solution.py:66
  1197.7 90.0 %all-gather.41.cloned.1.call-start = ((), (), s32[]{:S(2)}) async-start(), calls=%async_computation.45 | async-start | bytes 4718592 | tf_op jit(solution)/shard_map/all_gather | solution.py:74
  1249.2 116.1 %reduce-scatter.48.cloned.1.call-start = ((), (), s32[]{:S(2)}) async-start(), calls=%async_computation.46 | async-start | bytes 4718592 | tf_op jit(solution)/shard_map/reduce_scatter | solution.py:66
  1313.8 90.3 %all-gather.43.cloned.1.call-start = ((), (), s32[]{:S(2)}) async-start(), calls=%async_computation.47 | async-start | bytes 4718592 | tf_op jit(solution)/shard_map/all_gather | solution.py:74
  1365.4 114.9 %reduce-scatter.50.cloned.1.call-start = ((), (), s32[]{:S(2)}) async-start(), calls=%async_computation.48 | async-start | bytes 4718592 | tf_op jit(solution)/shard_map/reduce_scatter | solution.py:66
  1428.8 90.1 %all-gather.45.cloned.1.call-start = ((), (), s32[]{:S(2)}) async-start(), calls=%async_computation.49 | async-start | bytes 4718592 | tf_op jit(solution)/shard_map/all_gather | solution.py:74
  1480.3 127.8 %reduce-scatter.32.cloned.1.call-start = ((), (), s32[]{:S(2)}) async-start(), calls=%async_computation.35 | async-start | bytes 3276800 | tf_op jit(solution)/shard_map/reduce_scatter | solution.py:263
  1484.9 177.6 %reduce-scatter.28.cloned.1.call-start = ((), (), s32[]{:S(2)}) async-start(), calls=%async_computation.32 | async-start | bytes 3276800 | tf_op jit(solution)/shard_map/reduce_scatter | solution.py:263
  1536.8 125.7 %copy-start.5 = (bf16[2,2,80,1024]{3,2,1,0:T(8,128)(2,1)S(1)}, bf16[2,2,80,1024]{3,2,1,0:T(8,128)(2,1)}, u32[]{:S(2)}) copy-start(bf16[2,2,80,1024]{3,2,1,0:T(8,128)(2,1)} %param.23) | copy-start | bytes 1966084
  1536.8 125.7 %copy-start.53 = (f32[1,1024]{1,0:T(1,128)S(1)}, f32[1,1024]{1,0:T(1,128)}, u32[]{:S(2)}) copy-start(f32[1,1024]{1,0:T(1,128)} %copy-done.52) | copy-start | bytes 12292
  1536.8 125.7 %copy-start.55 = (f32[2,80]{1,0:T(2,128)S(1)}, f32[2,80]{1,0:T(2,128)}, u32[]{:S(2)}) copy-start(f32[2,80]{1,0:T(2,128)} %copy-done.54) | copy-start | bytes 1924
  1536.8 125.7 %copy-start.57 = (f32[2,80]{1,0:T(2,128)S(1)}, f32[2,80]{1,0:T(2,128)}, u32[]{:S(2)}) copy-start(f32[2,80]{1,0:T(2,128)} %copy-done.56) | copy-start | bytes 1924
  1536.8 127.4 %copy-start.77 = (f32[2,80]{1,0:T(2,128)S(1)}, f32[2,80]{1,0:T(2,128)}, u32[]{:S(2)}) copy-start(f32[2,80]{1,0:T(2,128)} %copy-done.76) | copy-start | bytes 1924
  1536.8 127.4 %copy-start.75 = (f32[2,80]{1,0:T(2,128)S(1)}, f32[2,80]{1,0:T(2,128)}, u32[]{:S(2)}) copy-start(f32[2,80]{1,0:T(2,128)} %copy-done.74) | copy-start | bytes 1924
  1536.8 127.5 %copy-start.71 = (f32[2,80]{1,0:T(2,128)S(1)}, f32[2,80]{1,0:T(2,128)}, u32[]{:S(2)}) copy-start(f32[2,80]{1,0:T(2,128)} %copy-done.70) | copy-start | bytes 1924
  1536.8 127.4 %copy-start.73 = (f32[2,80]{1,0:T(2,128)S(1)}, f32[2,80]{1,0:T(2,128)}, u32[]{:S(2)}) copy-start(f32[2,80]{1,0:T(2,128)} %copy-done.72) | copy-start | bytes 1924
  1536.8 175.8 %all-to-all-start.1 = ((f32[4,128,1024]{2,1,0:T(8,128)}), f32[4,128,1024]{2,1,0:T(8,128)}, u32[]{:S(2)}, u32[]{:S(2)}) async-start(f32[4,128,1024]{2,1,0:T(8,128)} %bitcast.417), calls=%async_computation.18 | async-start | bytes 4194304 | tf_op jit(solution)/shard_map/all_to_all | solution.py:305
  1542.1 124.2 %copy-start.60 = (f32[1024]{0:T(1024)S(1)}, f32[1024]{0:T(1024)}, u32[]{:S(2)}) copy-start(f32[1024]{0:T(1024)} %get-tuple-element.94) | copy-start | bytes 12292
  1542.1 164.9 %copy-start.12 = (f32[2,80,1024]{2,1,0:T(8,128)S(1)}, f32[2,80,1024]{2,1,0:T(8,128)}, u32[]{:S(2)}) copy-start(f32[2,80,1024]{2,1,0:T(8,128)} %copy-done.11) | copy-start | bytes 1966084
  1542.1 164.9 %copy-start.79 = (f32[2,80]{1,0:T(2,128)S(1)}, f32[2,80]{1,0:T(2,128)}, u32[]{:S(2)}) copy-start(f32[2,80]{1,0:T(2,128)} %copy-done.78) | copy-start | bytes 1924
  1542.1 164.9 %copy-start.81 = (f32[2,80]{1,0:T(2,128)S(1)}, f32[2,80]{1,0:T(2,128)}, u32[]{:S(2)}) copy-start(f32[2,80]{1,0:T(2,128)} %copy-done.80) | copy-start | bytes 1924
  (87 other events, 2089.2 us)
Sparse Core Ops, SparseCore 0:
  14.2 33.1 all-gather.28
  49.8 25.3 all-gather.20
  77.4 31.9 all-gather.18
  111.6 50.9 reduce-scatter.21
  164.7 51.7 reduce-scatter.17
  218.9 28.4 all-gather.24
  249.5 31.9 all-gather.30
  283.7 31.6 all-gather.22
  317.5 31.6 all-gather.48
  351.6 27.5 all-gather.26
  381.4 31.9 all-gather.46
  415.5 50.9 reduce-scatter.29
  468.8 51.7 reduce-scatter.25
  522.8 51.7 reduce-scatter.19
  576.8 51.7 reduce-scatter.23
  634.3 32.4 all-gather.34
  668.8 31.6 all-gather.32
  704.4 51.0 reduce-scatter.37
  759.8 51.3 reduce-scatter.39
  814.7 36.0 reduce-scatter.35
  854.7 46.2 reduce-scatter.33
  962.9 50.8 reduce-scatter.41
  1015.7 36.6 all-gather.36
  1080.9 51.3 reduce-scatter.43
  1134.3 36.6 all-gather.38
  1197.8 51.3 reduce-scatter.45
  1250.9 36.6 all-gather.40
  1314.0 51.3 reduce-scatter.47
  1367.4 36.6 all-gather.42
  1428.9 51.3 reduce-scatter.49
  1482.2 36.6 all-gather.44
  1521.2 86.8 reduce-scatter.31
  1610.2 52.2 reduce-scatter.27
where the time goes:
time: 1740 us; the launch traced here: 1730 us
  waiting for transfers between devices  1280 us (74%)
  matrix products  236 us (14%)
  blocking collectives  102 us (6%)
  other arithmetic  62.5 us (4%)
  local copies, waits for them, and re-layouts  21.3 us (1%)
    reduce_scatter x5, waiting for transfers between devices, gram_whole(): lax.psum_scatter(precise('rm,rn->mn', lax.slice_in_dim(matrix, 0, own_row...  257 us
    all_gather x5, waiting for transfers between devices, gram_whole(): return lax.all_gather(shard_rows, 'dp', axis=0, tiled=True)  180 us
    dot_general x15, matrix products, precise(): return jnp.einsum(form, left, right, precision=lax.Precision.HIGHEST)  125 us
    reduce_scatter x2, waiting for transfers between devices, per_device(): lax.psum_scatter(first_part, 'tensor', scatter_dimension=1, tiled=True)  120 us
    reduce_scatter x2, waiting for transfers between devices, per_device(): lax.psum_scatter(part_two, 'tensor', scatter_dimension=1, tiled=True)  106 us
    reduce_scatter x2, waiting for transfers between devices, per_device(): lax.psum_scatter(part_sum, 'tensor', scatter_dimension=1, tiled=True)  93.2 us
    reduce_scatter x2, waiting for transfers between devices, per_device(): lax.psum_scatter(second_part, 'tensor', scatter_dimension=1, tiled=True)  86.2 us
    all_gather x2, waiting for transfers between devices, per_device(): second_norm = lax.all_gather(second_local, 'tensor', axis=1, tiled=True)  63 us
  transfers between devices with their start and end apart: 34, of which 33 were waited for; matrix products, arithmetic and copies ran while one was open for 10% of the time, Pallas kernels for 0%

commit v1 on v0

--- a/solution.py
+++ b/solution.py
@@ -1,6 +1,10 @@
+import functools
+
 import jax
 import jax.numpy as jnp
 from jax import lax
+from jax.experimental import pallas as pl
+from jax.experimental.pallas import tpu as pltpu
 from jax.sharding import PartitionSpec as P
 
 HEAD_DIM = 64
@@ -369,6 +373,915 @@
     )
 
 
+MESH = pl.DeviceIdType.MESH
+BF = jnp.bfloat16
+F32 = jnp.float32
+VMEM_LIMIT = 60 * 1024 * 1024
+
+
+def place():
+    d = lax.axis_index("dp")
+    z = lax.axis_index("tensor")
+    y, x, c = d // 4, (d // 2) % 2, d % 2
+    return d, z, y, x, c
+
+
+def partners(d, z, y, x, c):
+    core = (d + 1 - 2 * c, z)
+    xn = (d + 2 - 4 * x, z)
+    yn = (d + 4 - 8 * y, z)
+    zn = [(d, (z + k) % 4) for k in range(1, 4)]
+    return core, xn, yn, zn
+
+
+def greet(others):
+    barrier = pltpu.get_barrier_semaphore()
+    for other in others:
+        pl.semaphore_signal(barrier, inc=1, device_id=other, device_id_type=MESH)
+    pl.semaphore_wait(barrier, len(others))
+
+
+def push(src, dst, sems, to):
+    return pltpu.make_async_remote_copy(
+        src_ref=src, dst_ref=dst, send_sem=sems[0], recv_sem=sems[1], device_id=to, device_id_type=MESH
+    )
+
+
+def gather_kernel(sizes, order, *refs):
+    n = len(sizes)
+    w = refs[:n]
+    tok, cot = refs[n : n + 2]
+    mom = refs[n + 2 : 2 * n + 2]
+    full = refs[2 * n + 2 : 3 * n + 2]
+    tok_all, cot_all, mom_all = refs[3 * n + 2 : 3 * n + 5]
+    z_s, z_r, loc, t_s, t_r, m_s, m_r, p_s, p_r = refs[3 * n + 5 :]
+    d, z, y, x, c = place()
+    core, xn, yn, zn = partners(d, z, y, x, c)
+    greet([core, xn, yn] + zn)
+    held = []
+
+    def start(copy):
+        copy.start()
+        held.append(copy)
+        return copy
+
+    def z_push(m):
+        for k in range(1, 4):
+            start(push(w[m], full[m].at[z, y, x, c], (z_s.at[m, k - 1], z_r.at[m, k - 1]), zn[k - 1]))
+
+    def z_wait(m, k):
+        slot = full[m].at[(z + 4 - k) % 4, y, x, c]
+        push(slot, slot, (z_s.at[m, k - 1], z_r.at[m, k - 1]), zn[k - 1]).wait_recv()
+
+    locals_ = []
+    for m in range(n):
+        copy = pltpu.make_async_copy(w[m], full[m].at[z, y, x, c], loc.at[m])
+        copy.start()
+        locals_.append(copy)
+    for i, (a, b) in enumerate(((tok, tok_all), (cot, cot_all))):
+        copy = pltpu.make_async_copy(a.at[z], b.at[z], loc.at[n + i])
+        copy.start()
+        locals_.append(copy)
+    z_push(0)
+
+    def rows_push(i, a, b):
+        for k in range(1, 4):
+            start(push(a.at[(z + k) % 4], b.at[z], (t_s.at[i, k - 1], t_r.at[i, k - 1]), zn[k - 1]))
+
+    def mom_push():
+        for t in range(n):
+            here = mom_all.at[z, pl.ds(0, sizes[t])]
+
+            @pl.when(z == t)
+            def _(t=t, here=here):
+                pltpu.make_async_copy(mom[t], here, loc.at[n + 2]).start()
+
+            @pl.when(z != t)
+            def _(t=t, here=here):
+                push(mom[t], here, (m_s.at[t], m_r.at[z]), (d, t)).start()
+
+    def mom_wait():
+        for t in range(n):
+            here = mom_all.at[z, pl.ds(0, sizes[t])]
+
+            @pl.when(z == t)
+            def _(t=t, here=here):
+                pltpu.make_async_copy(mom[t], here, loc.at[n + 2]).wait()
+                for k in range(1, 4):
+                    s = (t + k) % 4
+                    there = mom_all.at[s, pl.ds(0, sizes[t])]
+                    push(mom[t], there, (m_s.at[t], m_r.at[s]), (d, s)).wait_recv()
+
+            @pl.when(z != t)
+            def _(t=t, here=here):
+                push(mom[t], here, (m_s.at[t], m_r.at[z]), (d, t)).wait_send()
+
+    def sem(i, stage):
+        return (p_s.at[stage, i], p_r.at[stage, i])
+
+    def one(i):
+        m, k = order[i]
+        h = sizes[m] // 2
+        if k > 0:
+            z_wait(m, k)
+        else:
+            locals_[m].wait()
+        s = (z + 4 - k) % 4
+        a = full[m].at[s, y, x, c, pl.ds(0, h)]
+        b = full[m].at[s, y, x, c, pl.ds(h, h)]
+        start(push(a, a, sem(i, 0), xn))
+        start(push(b, b, sem(i, 1), yn))
+
+    def two(i):
+        m, k = order[i]
+        h = sizes[m] // 2
+        s = (z + 4 - k) % 4
+        a = full[m].at[s, y, 1 - x, c, pl.ds(0, h)]
+        push(a, a, sem(i, 0), xn).wait_recv()
+        a = full[m].at[s, y, :, c, pl.ds(0, h)]
+        start(push(a, a, sem(i, 2), yn))
+        b = full[m].at[s, 1 - y, x, c, pl.ds(h, h)]
+        push(b, b, sem(i, 1), yn).wait_recv()
+        b = full[m].at[s, :, x, c, pl.ds(h, h)]
+        start(push(b, b, sem(i, 3), xn))
+
+    def three(i):
+        m, k = order[i]
+        h = sizes[m] // 2
+        s = (z + 4 - k) % 4
+        a = full[m].at[s, 1 - y, :, c, pl.ds(0, h)]
+        push(a, a, sem(i, 2), yn).wait_recv()
+        b = full[m].at[s, :, 1 - x, c, pl.ds(h, h)]
+        push(b, b, sem(i, 3), xn).wait_recv()
+        e = full[m].at[s, :, :, c]
+        start(push(e, e, sem(i, 4), core))
+
+    count = len(order)
+    for i in range(count + 2):
+        if i < count:
+            one(i)
+        if i == 0:
+            z_push(1)
+            rows_push(0, tok, tok_all)
+            z_push(2)
+        if i == 5:
+            z_push(3)
+            rows_push(1, cot, cot_all)
+            mom_push()
+        if 1 <= i <= count:
+            two(i - 1)
+        if i >= 2:
+            three(i - 2)
+    for i in range(count):
+        m, k = order[i]
+        e = full[m].at[(z + 4 - k) % 4, :, :, 1 - c]
+        push(e, e, sem(i, 4), core).wait_recv()
+    for i, b in enumerate((tok_all, cot_all)):
+        locals_[n + i].wait()
+        for k in range(1, 4):
+            slot = b.at[(z + 4 - k) % 4]
+            push(slot, slot, (t_s.at[i, k - 1], t_r.at[i, k - 1]), zn[k - 1]).wait_recv()
+    mom_wait()
+    for copy in held:
+        copy.wait_send()
+
+
+def gather_all(weights, tok, cot, moms):
+    sizes = tuple(v.shape[0] for v in weights)
+    width = weights[0].shape[1]
+    order = [(0, 0), (1, 0), (2, 0), (0, 1), (0, 2), (0, 3), (1, 1), (1, 2), (1, 3)]
+    order += [(2, 1), (2, 2), (2, 3), (3, 0), (3, 1), (3, 2), (3, 3)]
+    count = len(order)
+    anyspace = pl.BlockSpec(memory_space=pl.ANY)
+    dma = pltpu.SemaphoreType.DMA
+    return pl.pallas_call(
+        functools.partial(gather_kernel, sizes, order),
+        out_shape=[jax.ShapeDtypeStruct((4, 2, 2, 2, s, width), BF) for s in sizes]
+        + [jax.ShapeDtypeStruct(tok.shape, BF), jax.ShapeDtypeStruct(cot.shape, BF)]
+        + [jax.ShapeDtypeStruct((4, max(sizes), width), BF)],
+        in_specs=[anyspace] * (2 * len(sizes) + 2),
+        out_specs=[anyspace] * (len(sizes) + 3),
+        scratch_shapes=[
+            dma((4, 3)),
+            dma((4, 3)),
+            dma((7,)),
+            dma((2, 3)),
+            dma((2, 3)),
+            dma((4,)),
+            dma((4,)),
+            dma((5, count)),
+            dma((5, count)),
+        ],
+        compiler_params=pltpu.CompilerParams(collective_id=1, has_side_effects=True, vmem_limit_bytes=8 << 20),
+    )(*weights, tok, cot, *moms)
+
+
+def add_rows(dst, src, lead, rows):
+    step = 16
+
+    def body(i, carry):
+        j, r = i // (rows // step), (i % (rows // step)) * step
+        at = pl.ds(pl.multiple_of(r, step), step)
+        dst[j, at] = dst[j, at] + src[j, at]
+        return carry
+
+    lax.fori_loop(0, lead * (rows // step), body, 0)
+
+
+def reduce_kernel(sizes, order, *refs):
+    n = len(sizes)
+    part = refs[:n]
+    small = refs[n]
+    total, small_out = refs[n + 1 : n + 3]
+    own = refs[n + 3 : 2 * n + 3]
+    got = refs[2 * n + 3 : 3 * n + 3]
+    mid = refs[3 * n + 3 : 4 * n + 3]
+    end = refs[4 * n + 3 : 5 * n + 3]
+    far, s_got, s_acc, s_z, loc, p_s, p_r, f_s, f_r, q_s, q_r = refs[5 * n + 3 :]
+    d, z, y, x, c = place()
+    core, xn, yn, zn = partners(d, z, y, x, c)
+    greet([core, xn, yn] + zn)
+    held = []
+
+    def start(copy):
+        copy.start()
+        held.append(copy)
+
+    def sem(i, stage):
+        return (p_s.at[stage, i], p_r.at[stage, i])
+
+    def zero(i):
+        m, k = order[i]
+        start(push(part[m].at[k, :, :, 1 - c], got[m].at[k], sem(i, 0), core))
+        pltpu.make_async_copy(part[m].at[k, :, :, c], own[m].at[k], loc.at[i]).start()
+
+    def one(i):
+        m, k = order[i]
+        s, h = sizes[m], sizes[m] // 2
+        pltpu.make_async_copy(part[m].at[k, :, :, c], own[m].at[k], loc.at[i]).wait()
+        push(part[m].at[k, :, :, 1 - c], got[m].at[k], sem(i, 0), core).wait_recv()
+        for j in range(2):
+            add_rows(own[m].at[k, j], got[m].at[k, j], 2, s)
+        start(push(own[m].at[k, 1 - y, :, pl.ds(0, h)], mid[m].at[k, 0], sem(i, 1), yn))
+        start(push(own[m].at[k, :, 1 - x, pl.ds(h, h)], mid[m].at[k, 1], sem(i, 2), xn))
+
+    def two(i):
+        m, k = order[i]
+        h = sizes[m] // 2
+        push(mid[m].at[k, 0], mid[m].at[k, 0], sem(i, 1), yn).wait_recv()
+        add_rows(own[m].at[k, y, :, pl.ds(0, h)], mid[m].at[k, 0], 2, h)
+        start(push(own[m].at[k, y, 1 - x, pl.ds(0, h)], end[m].at[k, pl.ds(0, h)], sem(i, 3), xn))
+        push(mid[m].at[k, 1], mid[m].at[k, 1], sem(i, 2), xn).wait_recv()
+        add_rows(own[m].at[k, :, x, pl.ds(h, h)], mid[m].at[k, 1], 2, h)
+        start(push(own[m].at[k, 1 - y, x, pl.ds(h, h)], end[m].at[k, pl.ds(h, h)], sem(i, 4), yn))
+
+    def three(i):
+        m, k = order[i]
+        s, h = sizes[m], sizes[m] // 2
+        push(end[m].at[k, pl.ds(0, h)], end[m].at[k, pl.ds(0, h)], sem(i, 3), xn).wait_recv()
+        push(end[m].at[k, pl.ds(h, h)], end[m].at[k, pl.ds(h, h)], sem(i, 4), yn).wait_recv()
+        add_rows(own[m].at[k, pl.ds(y, 1), x], end[m].at[pl.ds(k, 1)], 1, s)
+
+        @pl.when(z != m)
+        def _():
+            push(own[m].at[k, y, x], far.at[z, k, pl.ds(0, s)], (f_s.at[m, k], f_r.at[z, k]), (d, m)).start()
+
+    def four(i):
+        m, k = order[i]
+        s = sizes[m]
+
+        @pl.when(z == m)
+        def _():
+            for j in range(1, 4):
+                v = (m + j) % 4
+                slot = far.at[v, k, pl.ds(0, s)]
+                push(slot, slot, (f_s.at[m, k], f_r.at[v, k]), (d, v)).wait_recv()
+
+            def body(r, carry):
+                at = pl.ds(pl.multiple_of(r * 16, 16), 16)
+                acc = own[m][k, y, x, at].astype(F32)
+                for j in range(1, 4):
+                    acc = acc + far[(m + j) % 4, k, at].astype(F32)
+                total[k, at] = acc
+                return carry
+
+            lax.fori_loop(0, s // 16, body, 0)
+            if s < total.shape[1]:
+                total[k, pl.ds(s, total.shape[1] - s)] = jnp.zeros((total.shape[1] - s, total.shape[2]), F32)
+
+    def small_step(stage):
+        to = (core, xn, yn)
+        if stage > 0:
+            here = s_got.at[stage - 1]
+            push(here, here, (q_s.at[stage - 1], q_r.at[stage - 1]), to[stage - 1]).wait_recv()
+            s_acc[stage] = s_acc[stage - 1] + s_got[stage - 1]
+        else:
+            s_acc[0] = small[...]
+        if stage < 3:
+            start(push(s_acc.at[stage], s_got.at[stage], (q_s.at[stage], q_r.at[stage]), to[stage]))
+        else:
+            s_z[z] = s_acc[3]
+            for k in range(1, 4):
+                start(push(s_acc.at[3], s_z.at[z], (q_s.at[2 + k], q_r.at[2 + k]), zn[k - 1]))
+
+    count = len(order)
+    lead = 4
+    for i in range(lead):
+        zero(i)
+    small_step(0)
+    for i in range(count + 4):
+        if i + lead < count:
+            zero(i + lead)
+        if i < count:
+            one(i)
+        if 1 <= i <= count:
+            two(i - 1)
+        if 2 <= i <= count + 1:
+            three(i - 2)
+        if 4 <= i:
+            four(i - 4)
+        if i in (2, 4, 6):
+            small_step(i // 2)
+    for k in range(1, 4):
+        slot = s_z.at[(z + 4 - k) % 4]
+        push(slot, slot, (q_s.at[2 + k], q_r.at[2 + k]), zn[k - 1]).wait_recv()
+    small_out[...] = s_z[0] + s_z[1] + s_z[2] + s_z[3]
+    for copy in held:
+        copy.wait_send()
+    for m, k in order:
+
+        @pl.when(z != m)
+        def _(m=m, k=k):
+            slot = own[m].at[k, y, x]
+            push(slot, slot, (f_s.at[m, k], f_r.at[z, k]), (d, m)).wait_send()
+
+
+def reduce_all(parts, small):
+    sizes = tuple(v.shape[4] for v in parts)
+    width = parts[0].shape[5]
+    top = max(sizes)
+    order = [(m, k) for m in (3, 2, 1, 0) for k in range(4)]
+    count = len(order)
+    anyspace = pl.BlockSpec(memory_space=pl.ANY)
+    vmem = pl.BlockSpec(memory_space=pltpu.VMEM)
+    dma = pltpu.SemaphoreType.DMA
+    return pl.pallas_call(
+        functools.partial(reduce_kernel, sizes, order),
+        out_shape=[jax.ShapeDtypeStruct((4, top, width), F32), jax.ShapeDtypeStruct(small.shape, F32)],
+        in_specs=[anyspace] * len(sizes) + [vmem],
+        out_specs=[vmem, vmem],
+        scratch_shapes=[pltpu.VMEM((4, 2, 2, s, width), BF) for s in sizes]
+        + [pltpu.VMEM((4, 2, 2, s, width), BF) for s in sizes]
+        + [pltpu.VMEM((4, 2, 2, s // 2, width), BF) for s in sizes]
+        + [pltpu.VMEM((4, s, width), BF) for s in sizes]
+        + [
+            pltpu.VMEM((4, 4, top, width), BF),
+            pltpu.VMEM((3,) + small.shape, F32),
+            pltpu.VMEM((4,) + small.shape, F32),
+            pltpu.VMEM((4,) + small.shape, F32),
+            dma((count,)),
+            dma((5, count)),
+            dma((5, count)),
+            dma((4, 4)),
+            dma((4, 4)),
+            dma((6,)),
+            dma((6,)),
+        ],
+        compiler_params=pltpu.CompilerParams(collective_id=2, has_side_effects=True, vmem_limit_bytes=VMEM_LIMIT),
+    )(*parts, small)
+
+
+def gram_kernel(sizes, *refs):
+    n = len(sizes)
+    total, mom, outp, tokg = refs[:4]
+    gram, upd, upl = refs[4:7]
+    grads = refs[7 : 7 + n]
+    outp_all, tokg_all = refs[7 + n : 9 + n]
+    low_g, part, r_core, r_one, r_two, g_s, g_r, a_s, a_r, o_s, o_r, loc = refs[9 + n :]
+    d, z, y, x, c = place()
+    core, xn, yn, zn = partners(d, z, y, x, c)
+    greet([core, xn, yn] + zn)
+    held = []
+
+    def start(copy):
+        copy.start()
+        held.append(copy)
+
+    width = total.shape[2]
+    top = total.shape[1]
+    def cast(i, carry):
+        at = pl.ds(pl.multiple_of((i % (top // 16)) * 16, 16), 16)
+        low_g[i // (top // 16), at] = total[i // (top // 16), at].astype(BF)
+        return carry
+
+    lax.fori_loop(0, 4 * (top // 16), cast, 0)
+    for t in range(n):
+
+        @pl.when(z == t)
+        def _(t=t):
+            s = sizes[t]
+            for k in range(1, 4):
+                v = (t + k) % 4
+                push(low_g.at[v, pl.ds(0, s)], grads[t], (g_s.at[v], g_r.at[t]), (d, v)).start()
+            pltpu.make_async_copy(low_g.at[t, pl.ds(0, s)], grads[t], loc.at[0]).start()
+
+    height = jnp.where(z == 0, sizes[0], jnp.where(z == 1, sizes[1], jnp.where(z == 2, sizes[2], sizes[3])))
+
+    def make(i, carry):
+        k, r = i // (top // 16), (i % (top // 16)) * 16
+        at = pl.ds(pl.multiple_of(r, 16), 16)
+        g = total[k, at]
+        u = g + muon_decay * (muon_decay * mom[k, at].astype(F32) + g)
+        row = lax.broadcasted_iota(jnp.int32, u.shape, 0) + r
+        u = jnp.where(row < height, u, 0.0)
+        hi = u.astype(BF)
+        to = pl.ds(pl.multiple_of(i * 16, 16), 16)
+        upd[to] = hi
+        upl[to] = (u - hi.astype(F32)).astype(BF)
+        return carry
+
+    lax.fori_loop(0, 4 * (top // 16), make, 0)
+    tile = 256
+    dims = (((0,), (0,)), ((), ()))
+
+    def mul(i, carry):
+        at = pl.ds(pl.multiple_of(i * tile, tile), tile)
+        hi, lo = upd[:, at], upl[:, at]
+        acc = lax.dot_general(upd[...], hi, dims, preferred_element_type=F32)
+        acc = acc + lax.dot_general(upd[...], lo, dims, preferred_element_type=F32)
+        part[:, at] = acc + lax.dot_general(upl[...], hi, dims, preferred_element_type=F32)
+        return carry
+
+    lax.fori_loop(0, width // tile, mul, 0)
+
+    def add(dst, r0, src, rows, into=None, r1=None):
+        def body(i, carry):
+            at = pl.ds(pl.multiple_of(r0 + i * 8, 8), 8)
+            v = dst[at] + src[pl.ds(pl.multiple_of(i * 8, 8), 8)]
+            if into is None:
+                dst[at] = v
+            else:
+                into[at] = v
+            return carry
+
+        lax.fori_loop(0, rows // 8, body, 0)
+
+    half, quarter, eighth = width // 2, width // 8, width // 16
+
+    def sem(i):
+        return (a_s.at[i], a_r.at[i])
+
+    def rows(ref, r, count):
+        return ref.at[pl.ds(pl.multiple_of(r, 64), count)]
+
+    start(push(rows(part, (1 - c) * half, half), r_core, sem(0), core))
+    push(r_core, r_core, sem(0), core).wait_recv()
+    base_a = c * half
+    base_b = c * half + half // 2
+    add(part, base_a, r_core, half)
+    start(push(rows(part, base_a + (1 - y) * quarter, quarter), r_one.at[0], sem(1), yn))
+    start(push(rows(part, base_b + (1 - x) * quarter, quarter), r_one.at[1], sem(2), xn))
+    for i, (a, b) in enumerate(((outp, outp_all), (tokg, tokg_all))):
+        pltpu.make_async_copy(a.at[z], b.at[z], loc.at[1 + i]).start()
+        for k in range(1, 4):
+            start(push(a.at[(z + k) % 4], b.at[z], (o_s.at[i, k - 1], o_r.at[i, k - 1]), zn[k - 1]))
+    push(r_one.at[0], r_one.at[0], sem(1), yn).wait_recv()
+    mine_a = base_a + y * quarter
+    add(part, mine_a, r_one.at[0], quarter)
+    start(push(rows(part, mine_a + (1 - x) * eighth, eighth), r_two.at[0], sem(3), xn))
+    push(r_one.at[1], r_one.at[1], sem(2), xn).wait_recv()
+    mine_b = base_b + x * quarter
+    add(part, mine_b, r_one.at[1], quarter)
+    start(push(rows(part, mine_b + (1 - y) * eighth, eighth), r_two.at[1], sem(4), yn))
+    push(r_two.at[0], r_two.at[0], sem(3), xn).wait_recv()
+    own_a = mine_a + x * eighth
+    add(part, own_a, r_two.at[0], eighth, gram)
+    start(push(rows(gram, own_a, eighth), rows(gram, own_a, eighth), sem(5), xn))
+    push(r_two.at[1], r_two.at[1], sem(4), yn).wait_recv()
+    own_b = mine_b + y * eighth
+    add(part, own_b, r_two.at[1], eighth, gram)
+    start(push(rows(gram, own_b, eighth), rows(gram, own_b, eighth), sem(6), yn))
+    got_a = rows(gram, mine_a + (1 - x) * eighth, eighth)
+    push(got_a, got_a, sem(5), xn).wait_recv()
+    start(push(rows(gram, mine_a, quarter), rows(gram, mine_a, quarter), sem(7), yn))
+    got_b = rows(gram, mine_b + (1 - y) * eighth, eighth)
+    push(got_b, got_b, sem(6), yn).wait_recv()
+    start(push(rows(gram, mine_b, quarter), rows(gram, mine_b, quarter), sem(8), xn))
+    got_a = rows(gram, base_a + (1 - y) * quarter, quarter)
+    push(got_a, got_a, sem(7), yn).wait_recv()
+    start(push(rows(gram, base_a, half // 2), rows(gram, base_a, half // 2), sem(9), core))
+    got_b = rows(gram, base_b + (1 - x) * quarter, quarter)
+    push(got_b, got_b, sem(8), xn).wait_recv()
+    start(push(rows(gram, base_b, half // 2), rows(gram, base_b, half // 2), sem(10), core))
+    got_a = rows(gram, (1 - c) * half, half // 2)
+    push(got_a, got_a, sem(9), core).wait_recv()
+    got_b = rows(gram, (1 - c) * half + half // 2, half // 2)
+    push(got_b, got_b, sem(10), core).wait_recv()
+
+    for i, (a, b) in enumerate(((outp, outp_all), (tokg, tokg_all))):
+        pltpu.make_async_copy(a.at[z], b.at[z], loc.at[1 + i]).wait()
+        for k in range(1, 4):
+            slot = b.at[(z + 4 - k) % 4]
+            push(slot, slot, (o_s.at[i, k - 1], o_r.at[i, k - 1]), zn[k - 1]).wait_recv()
+    for t in range(n):
+        s = sizes[t]
+
+        @pl.when(z == t)
+        def _(t=t, s=s):
+            pltpu.make_async_copy(low_g.at[t, pl.ds(0, s)], grads[t], loc.at[0]).wait()
+            for k in range(1, 4):
+                v = (t + k) % 4
+                push(low_g.at[v, pl.ds(0, s)], grads[t], (g_s.at[v], g_r.at[t]), (d, v)).wait_send()
+
+        @pl.when(z != t)
+        def _(t=t):
+            push(grads[t], grads[t], (g_s.at[t], g_r.at[t]), (d, t)).wait_recv()
+    for copy in held:
+        copy.wait_send()
+
+
+def gram_all(total, mom, outp, tokg, sizes):
+    top, width = total.shape[1:]
+    anyspace = pl.BlockSpec(memory_space=pl.ANY)
+    vmem = pl.BlockSpec(memory_space=pltpu.VMEM)
+    dma = pltpu.SemaphoreType.DMA
+    return pl.pallas_call(
+        functools.partial(gram_kernel, sizes),
+        out_shape=[jax.ShapeDtypeStruct((width, width), F32)]
+        + [jax.ShapeDtypeStruct((4 * top, width), BF)] * 2
+        + [jax.ShapeDtypeStruct((s, width), BF) for s in sizes]
+        + [jax.ShapeDtypeStruct(outp.shape, outp.dtype), jax.ShapeDtypeStruct(tokg.shape, tokg.dtype)],
+        in_specs=[vmem, vmem, anyspace, anyspace],
+        out_specs=[vmem] * 3 + [anyspace] * (len(sizes) + 2),
+        scratch_shapes=[
+            pltpu.VMEM((4, top, width), BF),
+            pltpu.VMEM((width, width), F32),
+            pltpu.VMEM((width // 2, width), F32),
+            pltpu.VMEM((2, width // 8, width), F32),
+            pltpu.VMEM((2, width // 16, width), F32),
+            dma((4,)),
+            dma((4,)),
+            dma((11,)),
+            dma((11,)),
+            dma((2, 3)),
+            dma((2, 3)),
+            dma((3,)),
+        ],
+        compiler_params=pltpu.CompilerParams(collective_id=3, has_side_effects=True, vmem_limit_bytes=VMEM_LIMIT),
+    )(total, mom, outp, tokg)
+
+
+def split(v):
+    hi = v.astype(BF)
+    return hi, (v - hi.astype(F32)).astype(BF)
+
+
+def dot(a, b):
+    return jnp.dot(a, b, preferred_element_type=F32)
+
+
+def polish_kernel(gram, hi, lo, out, gf, gh, gl, low, b, xf, xh, xl):
+    width = gram.shape[0]
+    rows = hi.shape[0]
+    tile = 256
+    step = 64
+    eye = jnp.where(
+        lax.broadcasted_iota(jnp.int32, (128, 128), 0) == lax.broadcasted_iota(jnp.int32, (128, 128), 1), 1.0, 0.0
+    ).astype(F32)
+    trace = jnp.zeros((1, 1), F32)
+    for i in range(width // 128):
+        block = gram[i * 128 : (i + 1) * 128, i * 128 : (i + 1) * 128] * eye
+        trace = trace + jnp.sum(jnp.sum(block, axis=1, keepdims=True), axis=0, keepdims=True)
+    inverse = 1.0 / (jnp.sqrt(trace) + frob_eps)
+    squared = inverse * inverse
+
+    def scale_gram(i, carry):
+        at = pl.ds(pl.multiple_of(i * step, step), step)
+        v = gram[at] * squared
+        gf[at] = v
+        gh[at], gl[at] = split(v)
+        return carry
+
+    lax.fori_loop(0, width // step, scale_gram, 0)
+
+    def scale_x(i, carry):
+        at = pl.ds(pl.multiple_of(i * step, step), step)
+        v = (hi[at].astype(F32) + lo[at].astype(F32)) * inverse
+        xf[at] = v
+        xh[at], xl[at] = split(v)
+        return carry
+
+    lax.fori_loop(0, rows // step, scale_x, 0)
+
+    def columns(i):
+        return pl.ds(pl.multiple_of(i * tile, tile), tile)
+
+    def iterate(shift, double, last):
+        level = coef_a + coef_b * shift + coef_c * shift * shift
+        slope = coef_b + 2.0 * coef_c * shift
+        left = low if last else gh
+
+        def poly(i, carry):
+            at = columns(i)
+            g = gf[:, at]
+            if last:
+                row = lax.broadcasted_iota(jnp.int32, g.shape, 0)
+                col = lax.broadcasted_iota(jnp.int32, g.shape, 1) + i * tile
+                g = g - jnp.where(row == col, shift, 0.0)
+            b[:, at] = (slope * g + coef_c * dot(left[...], left[:, at])).astype(BF)
+            return carry
+
+        if last:
+
+            def lower(i, carry):
+                at = pl.ds(pl.multiple_of(i * step, step), step)
+                g = gf[at]
+                row = lax.broadcasted_iota(jnp.int32, g.shape, 0) + i * step
+                col = lax.broadcasted_iota(jnp.int32, g.shape, 1)
+                low[at] = (g - jnp.where(row == col, shift, 0.0)).astype(BF)
+                return carry
+
+            lax.fori_loop(0, width // step, lower, 0)
+        lax.fori_loop(0, width // tile, poly, 0)
+
+        def apply(i, carry):
+            at = columns(i)
+            right = b[:, at]
+            v = level * xf[:, at] + dot(xh[...], right)
+            if double:
+                v = v + dot(xl[...], right)
+            if last:
+                out[:, at] = v.astype(BF)
+                return carry
+            xf[:, at] = v
+            t = level * gf[:, at] + dot(gh[...], right)
+            if double:
+                t = t + dot(gl[...], right)
+                th, tl = split(t)
+                gf[:, at] = level * t + dot(b[...], th) + dot(b[...], tl)
+            else:
+                gf[:, at] = level * t + dot(b[...], t.astype(BF))
+            return carry
+
+        lax.fori_loop(0, width // tile, apply, 0)
+        if not last:
+
+            def lower_g(i, carry):
+                at = pl.ds(pl.multiple_of(i * step, step), step)
+                gh[at] = gf[at].astype(BF)
+                return carry
+
+            lax.fori_loop(0, width // step, lower_g, 0)
+
+            def lower_x(i, carry):
+                at = pl.ds(pl.multiple_of(i * step, step), step)
+                xh[at] = xf[at].astype(BF)
+                return carry
+
+            lax.fori_loop(0, rows // step, lower_x, 0)
+
+    iterate(0.0, True, False)
+
+    def middle(i, carry):
+        iterate(0.0, False, False)
+        return carry
+
+    lax.fori_loop(0, NS_STEPS - 2, middle, 0)
+    iterate(0.8, False, True)
+
+
+def polish(gram, hi, lo):
+    rows, width = hi.shape
+    vmem = pl.BlockSpec(memory_space=pltpu.VMEM)
+    return pl.pallas_call(
+        polish_kernel,
+        out_shape=jax.ShapeDtypeStruct((rows, width), BF),
+        in_specs=[vmem] * 3,
+        out_specs=vmem,
+        scratch_shapes=[pltpu.VMEM((width, width), F32)]
+        + [pltpu.VMEM((width, width), BF)] * 4
+        + [pltpu.VMEM((rows, width), F32)]
+        + [pltpu.VMEM((rows, width), BF)] * 2,
+        compiler_params=pltpu.CompilerParams(vmem_limit_bytes=VMEM_LIMIT),
+        cost_estimate=pl.CostEstimate(flops=39 * 10**9, bytes_accessed=8 * 10**6, transcendentals=0),
+    )(gram, hi, lo)
+
+
+def return_kernel(sizes, *refs):
+    n = len(sizes)
+    done = refs[0]
+    rows = refs[1 : 1 + n]
+    s_s, s_r, loc = refs[1 + n :]
+    d, z, y, x, c = place()
+    core, xn, yn, zn = partners(d, z, y, x, c)
+    greet(zn)
+    for t in range(n):
+        s = sizes[t]
+
+        @pl.when(z == t)
+        def _(t=t, s=s):
+            for k in range(1, 4):
+                v = (t + k) % 4
+                push(done.at[v, pl.ds(0, s)], rows[t], (s_s.at[v], s_r.at[t]), (d, v)).start()
+            pltpu.make_async_copy(done.at[t, pl.ds(0, s)], rows[t], loc.at[0]).start()
+
+    for t in range(n):
+        s = sizes[t]
+
+        @pl.when(z == t)
+        def _(t=t, s=s):
+            pltpu.make_async_copy(done.at[t, pl.ds(0, s)], rows[t], loc.at[0]).wait()
+            for k in range(1, 4):
+                v = (t + k) % 4
+                push(done.at[v, pl.ds(0, s)], rows[t], (s_s.at[v], s_r.at[t]), (d, v)).wait_send()
+
+        @pl.when(z != t)
+        def _(t=t):
+            push(rows[t], rows[t], (s_s.at[t], s_r.at[t]), (d, t)).wait_recv()
+
+
+def return_all(done, sizes):
+    anyspace = pl.BlockSpec(memory_space=pl.ANY)
+    dma = pltpu.SemaphoreType.DMA
+    return pl.pallas_call(
+        functools.partial(return_kernel, sizes),
+        out_shape=[jax.ShapeDtypeStruct((s, done.shape[2]), BF) for s in sizes],
+        in_specs=[anyspace],
+        out_specs=[anyspace] * len(sizes),
+        scratch_shapes=[dma((4,)), dma((4,)), dma((1,))],
+        compiler_params=pltpu.CompilerParams(collective_id=4, has_side_effects=True, vmem_limit_bytes=8 << 20),
+    )(done)
+
+
+def whole_image(x, cot, live, weights, head_bias, expand_bias, norm_gain, model_bias):
+    intake, outlet, expand, shrink = weights
+    seq, width = x.shape
+    heads = width // HEAD_DIM
+    scale = HEAD_DIM ** (-0.5)
+    query_bias = head_bias[0].reshape(heads, HEAD_DIM)
+    value_bias = head_bias[1].reshape(heads, HEAD_DIM)
+    mixed_bias = jnp.stack([query_bias, jnp.zeros_like(query_bias), value_bias], axis=1).reshape(3 * width)
+
+    def ein(form, a, b):
+        return jnp.einsum(form, a, b, preferred_element_type=F32)
+
+    def norm(v, g, s):
+        center = v - jnp.mean(v, axis=-1, keepdims=True)
+        r = lax.rsqrt(jnp.mean(center * center, axis=-1, keepdims=True) + norm_eps)
+        n = center * r
+        return n * g + s, n, r
+
+    def norm_back(n, r, g, w):
+        u = w * g
+        down = r * (u - jnp.mean(u, axis=-1, keepdims=True) - n * jnp.mean(u * n, axis=-1, keepdims=True))
+        return down, jnp.sum(w * n, axis=0), jnp.sum(w, axis=0)
+
+    rows = x.astype(F32)
+    first, n1, r1 = norm(rows, norm_gain[0], model_bias[0])
+    first = first.astype(BF)
+    mixed = (ein("sd,rd->sr", first, intake) + mixed_bias).astype(BF).reshape(seq, heads, 3, HEAD_DIM)
+    q, k, v = mixed[:, :, 0], mixed[:, :, 1], mixed[:, :, 2]
+    scores = ein("qhe,khe->hqk", q, k) * scale
+    scores = jnp.where(live[None, None, :], scores, masked_score)
+    attention = softmax_rows(scores)
+    attention16 = attention.astype(BF)
+    attended = ein("hqk,khe->qhe", attention16, v).reshape(seq, width).astype(BF)
+    middle = rows + ein("sc,cd->sd", attended, outlet) + model_bias[2]
+    second, n2, r2 = norm(middle, norm_gain[1], model_bias[1])
+    second = second.astype(BF)
+    hidden = ein("sd,fd->sf", second, expand) + expand_bias
+    bell = 0.5 * (1.0 + lax.erf(hidden * (0.5**0.5)))
+    active = (hidden * bell).astype(BF)
+    output = middle + ein("sf,fd->sd", active, shrink) + model_bias[3]
+    shrink_grad = ein("sf,sd->fd", active, cot)
+    active_grad = ein("sd,fd->sf", cot, shrink)
+    slope = bell + hidden * jnp.exp(-0.5 * hidden * hidden) * (0.5 / jnp.pi) ** 0.5
+    hidden_grad = (active_grad * slope).astype(BF)
+    hidden_bias_grad = jnp.sum(hidden_grad.astype(F32), axis=0)
+    expand_grad = ein("sf,sd->fd", hidden_grad, second)
+    second_grad = ein("sf,fd->sd", hidden_grad, expand)
+    down, gain_two, shift_two = norm_back(n2, r2, norm_gain[1], second_grad)
+    cot_float = cot.astype(F32)
+    middle_grad = cot_float + down
+    branch = middle_grad.astype(BF)
+    outlet_grad = ein("sc,sd->cd", attended, branch)
+    attended_grad = ein("sd,cd->sc", branch, outlet).astype(BF).reshape(seq, heads, HEAD_DIM)
+    values_grad = ein("hqk,qhe->khe", attention16, attended_grad)
+    attention_grad = ein("qhe,khe->hqk", attended_grad, v)
+    score_grad = attention * (attention_grad - jnp.sum(attention_grad * attention, axis=-1, keepdims=True))
+    score_grad = score_grad.astype(BF)
+    queries_grad = ein("hqk,khe->qhe", score_grad, k) * scale
+    keys_grad = ein("hqk,qhe->khe", score_grad, q) * scale
+    mixed_grad = jnp.stack([queries_grad, keys_grad, values_grad], axis=2).astype(BF)
+    sums = jnp.sum(mixed_grad.astype(F32), axis=0)
+    mixed_grad = mixed_grad.reshape(seq, 3 * width)
+    intake_grad = ein("sr,sd->rd", mixed_grad, first)
+    first_grad = ein("sr,rd->sd", mixed_grad, intake)
+    down, gain_one, shift_one = norm_back(n1, r1, norm_gain[0], first_grad)
+    token_grad = middle_grad + down
+    small = jnp.concatenate(
+        [
+            sums[:, 0].reshape(1, width),
+            sums[:, 2].reshape(1, width),
+            hidden_bias_grad.reshape(-1, width),
+            gain_one[None],
+            gain_two[None],
+            shift_one[None],
+            shift_two[None],
+            jnp.sum(branch.astype(F32), axis=0)[None],
+            jnp.sum(cot_float, axis=0)[None],
+        ]
+    )
+    grads = tuple(g.astype(BF) for g in (intake_grad, outlet_grad, expand_grad, shrink_grad))
+    return output.astype(BF), token_grad.astype(BF), grads, small
+
+
+def per_device_fast(
+    tokens,
+    cotangent,
+    keep_mask,
+    intake,
+    outlet,
+    expand,
+    shrink,
+    intake_moment,
+    outlet_moment,
+    expand_moment,
+    shrink_moment,
+    head_bias,
+    expand_bias,
+    norm_gain,
+    model_bias,
+    head_first,
+    head_second,
+    expand_first,
+    expand_second,
+    gain_first,
+    gain_second,
+    bias_first,
+    bias_second,
+):
+    shape = tokens.shape
+    local, width = shape[2:]
+    z = lax.axis_index("tensor")
+    masters = (intake, outlet, expand, shrink)
+    moments = (intake_moment, outlet_moment, expand_moment, shrink_moment)
+    sizes = tuple(v.shape[0] for v in masters)
+    gathered = gather_all(
+        [v.astype(BF) for v in masters],
+        tokens.reshape(-1, local, width),
+        cotangent.reshape(-1, local, width),
+        [v.astype(BF) for v in moments],
+    )
+    whole = [v.reshape(-1, width) for v in gathered[:4]]
+    x, cot = (v.reshape(-1, width) for v in gathered[4:6])
+    seq = x.shape[0]
+    keep = lax.dynamic_index_in_dim(keep_mask.reshape(-1, seq), z, 0, keepdims=False)
+    live = jnp.logical_or(keep != 0, jnp.arange(seq) < BUF)
+    out, token_grad, grads, small = whole_image(
+        x, cot, live, whole, head_bias, expand_bias, norm_gain, model_bias
+    )
+    count = small.shape[0]
+    small = jnp.pad(small, ((0, -count % 8), (0, 0)))
+    parts = [g.reshape(4, 2, 2, 2, s, width) for g, s in zip(grads, sizes)]
+    total, small = reduce_all(parts, small)
+    made = gram_all(total, gathered[6], out.reshape(-1, local, width), token_grad.reshape(-1, local, width), sizes)
+    gram, hi, lo = made[:3]
+    shards = [g.astype(F32) for g in made[3:7]]
+    output = made[7].reshape(shape).astype(F32)
+    token_grad = made[8].reshape(shape).astype(F32)
+    done = polish(gram, hi, lo).reshape(4, -1, width)
+    returned = return_all(done, sizes)
+    head_total = small[0:2]
+    units = expand_bias.shape[0] // width
+    hidden_total = small[2 : 2 + units].reshape(expand_bias.shape)
+    gain_total = small[2 + units : 4 + units]
+    bias_total = small[4 + units : 8 + units]
+    moments_new = [muon_decay * moment + gradient for gradient, moment in zip(shards, moments)]
+    rows_scale = lax.axis_size("dp") * lax.axis_size("tensor")
+    masters_new = [
+        weight - rate * (weight.shape[0] * rows_scale / width) ** 0.5 * rows.astype(F32)
+        for weight, rate, rows in zip(masters, muon_rates, returned)
+    ]
+    head = adam_step(head_total, head_first, head_second)
+    hidden = adam_step(hidden_total, expand_first, expand_second)
+    gain = adam_step(gain_total, gain_first, gain_second)
+    bias = adam_step(bias_total, bias_first, bias_second)
+    return (
+        (output, token_grad)
+        + tuple(shards)
+        + (head_total, hidden_total, gain_total, bias_total)
+        + tuple(moments_new)
+        + tuple(masters_new)
+        + tuple(v.astype(BF) for v in masters_new)
+        + (head[0], hidden[0], gain[0], bias[0])
+        + head[1:]
+        + hidden[1:]
+        + gain[1:]
+        + bias[1:]
+    )
+
+
 def solution(mesh):
     placed = (
         P(None, "dp", "tensor", None),
@@ -395,8 +1308,9 @@
         P(),
         P(),
     )
+    fast = mesh.shape["dp"] == 8 and mesh.shape["tensor"] == 4
     return jax.shard_map(
-        per_device,
+        per_device_fast if fast else per_device,
         mesh=mesh,
         in_specs=placed,
         out_specs=(

time: 1740 us -> 630 us (0.36)
  waiting for transfers between devices: 1280 us -> 0 us
  Pallas kernels: 0 us -> 482 us
  matrix products: 236 us -> 88.9 us
  blocking collectives: 102 us -> 0 us
  other arithmetic: 62.5 us -> 29.7 us
    reduce_scatter x17 -> x0, waiting for transfers between devices: 826 us -> none  [the longest x5 257 us: gram_whole(): lax.psum_scatter(precise('rm,rn->mn', lax.slice_in_dim(matrix, 0, own_row...]
    pallas_call x0 -> x5, Pallas kernels: none -> 482 us  [the longest x1 188 us: reduce_all(): pl.pallas_call(functools.partial(reduce_kernel, sizes, order), out_shape=...]
    all_gather x16 -> x0, waiting for transfers between devices: 450 us -> none  [the longest x5 180 us: gram_whole(): return lax.all_gather(shard_rows, 'dp', axis=0, tiled=True)]
    dot_general x49 -> x17, matrix products: 230 us -> 81.2 us  [ein(): return jnp.einsum(form, a, b, preferred_element_type=F32)]
    all_to_all x1 -> x0, blocking collectives: 51.3 us -> none  [per_device(): lax.all_to_all(padded, 'tensor', split_axis=0, concat_axis=0, tiled=True)]
    psum x1 -> x0, blocking collectives: 40.6 us -> none  [per_device(): lax.psum((gain_grad, bias_grad, head_full, hidden_full), ('dp', 'tensor'))]
  transfers between devices with their start and end apart: 34 -> 0, of which waited for: 33 -> 0; matrix products, arithmetic and copies ran while one was open for 10% -> 0% of each run, Pallas kernels for 0% -> 0%
where the time goes in v1:
time: 630 us; the launch traced here: 626 us
  Pallas kernels  482 us (77%)
  matrix products  88.9 us (14%)
  other arithmetic  29.7 us (5%)
  local copies, waits for them, and re-layouts  22.8 us (4%)
    pallas_call x1, Pallas kernels, reduce_all(): pl.pallas_call(functools.partial(reduce_kernel, sizes, order), out_shape=...  188 us
    pallas_call x1, Pallas kernels, gather_all(): pl.pallas_call(functools.partial(gather_kernel, sizes, order), out_shape=...  141 us
    dot_general x17, matrix products, ein(): return jnp.einsum(form, a, b, preferred_element_type=F32)  81.2 us
    pallas_call x1, Pallas kernels, polish(): pl.pallas_call(polish_kernel, out_shape=jax.ShapeDtypeStruct((rows, width...  64.8 us
    pallas_call x1, Pallas kernels, gram_all(): pl.pallas_call(functools.partial(gram_kernel, sizes), out_shape=[jax.Shap...  58.9 us
    pallas_call x1, Pallas kernels, return_all(): pl.pallas_call(functools.partial(return_kernel, sizes), out_shape=[jax.Sh...  29.7 us
    unnamed x126, local copies, waits for them, and re-layouts  15.2 us

profile of v1, /device:TPU:8, one launch (start us, length us, event | category | flops | bytes accessed | tf_op | source)
XLA Modules:
  0.0 625.7 jit_solution(13214335453034528285)
XLA Ops:
  0.8 1.2 convert_element_type.178.refs_2_
  2.0 1.1 convert_element_type.179.refs_3_
  3.1 1.1 convert_element_type.182.refs_8_
  4.4 140.9 %shard_map.486 = (bf16[4,2,2,2,96,1024]{5,4,3,2,1,0:T(8,128)(2,1)S(1)}, bf16[4,2,2,2,32,1024]{5,4,3,2,1,0:T(8,128)(2,1)S(1)}, bf16[4,2,2,2,128,1024]{5,4,3,2,1,0...) custom-call(bf16[96,1024]{1,0:T(8,128)(2,1)S(1)} %convert_element_ty, ...), custom_call_target="tpu_custom_call" | custom-call | tf_op jit(solution)/shard_map/pallas_call | solution.py:557
  145.3 2.7 copy-done
  148.0 1.0 copy-done.1
  149.0 3.3 copy-done.5
  152.2 3.2 copy-done.6
  156.1 1.2 add_convert_fusion.2
  157.6 6.5 %fusion.7 = bf16[320,3072]{1,0:T(8,128)(2,1)} fusion(bf16[320,1024]{1,0:T(8,128)(2,1)} %bitcast.171, bf16[3072,1024]{1,0:T(8,128)(2,1)} %bitcast.133, f32[3072]{0:T(1024)S(1)} %add.163), kind=kOutput, calls=%fused_computation.22 | convolution fusion | flops 2015232000 | bytes 8925184 | tf_op jit(solution)/shard_map/sd,rd->sr/dot_general | solution.py:1126
  164.2 4.6 copy.68
  168.8 7.7 %fusion.54 = (f32[16,320]{1,0:T(8,128)S(1)}, f32[16,320,320]{1,2,0:T(8,128)}) fusion(pred[320]{0:T(512)(128)(4,1)S(1)} %fusion.38, bf16[320,16,3,64]{0,3,2,1:T(8,128)(2,1)} %bitcast.159), kind=kOutput, calls=%fused_computation.121 | convolution fusion | flops 216269120 | bytes 8147264 | tf_op jit(solution)/shard_map/sub | solution.py:42
  176.5 4.4 fusion.16
  180.9 1.0 fusion.55
  182.2 7.9 %multiply_convert_fusion.1 = (bf16[320,4096]{1,0:T(8,128)(2,1)}, f32[320,4096]{1,0:T(8,128)S(1)}) fusion(f32[4096]{0:T(1024)S(1)} %copy-done.52, bf16[4096,1024]{1,0:T(8,128)(2,1)} %bitcast.150, f32[320,1024]{1,0:T(8,128)S(1)} %get-tuple-element.140, f32[1024]{0:T(1024)S(1)} %bitcast.192, f32[1024]{0:T(1024)S(1)} %bitcast.186, f32[320]{0:T(512)S(1)} %add_rsqrt_fusion, ...), kind=kOutput, calls=%fused_computation.18 | convolution fusion | flops 2693857280 | bytes 17590784 | tf_op jit(solution)/shard_map/sd,fd->sf/dot_general | solution.py:1126
  190.1 6.1 convert_reduce_fusion
  196.3 6.0 multiply_reduce_fusion.2
  202.5 3.4 convert_reduce_fusion.3
  205.9 1.1 copy-done.11
  206.9 1.7 convolution_convert_fusion.4
  208.7 1.4 copy.73
  210.1 8.1 %multiply_reduce_fusion = (f32[16,320]{1,0:T(8,128)S(1)}, f32[16,320,320]{1,2,0:T(8,128)}) fusion(f32[16,320,320]{1,2,0:T(8,128)} %get-tuple-element.138, f32[16,320]{1,0:T(8,128)S(1)} %get-tuple-element.137, bf16[320,16,64]{0,2,1:T(8,128)(2,1)S(1)} %bitcast.168, bf16[320,16,3,64]{0,3,2,1:T(8,128)(2,1)} %bitcast.161), kind=kOutput, calls=%fused_computation.2 | convolution fusion | flops 214625280 | bytes 15900672 | tf_op jit(solution)/shard_map/qhe,khe->hqk/dot_general | solution.py:1126
  218.2 7.0 %multiply_convert_fusion = bf16[16,320,320]{1,2,0:T(8,128)(2,1)S(1)} fusion(f32[16,320,320]{1,2,0:T(8,128)} %get-tuple-element.143, f32[16,320]{1,0:T(8,128)S(1)} %get-tuple-element.142, f32[16,320,320]{1,2,0:T(8,128)} %get-tuple-element.138, f32[16,320]{1,0:T(8,128)S(1)} %get-tuple-element.137), kind=kLoop, calls=%fused_computation.1 | loop fusion | flops 6553600 | bytes 16424960 | tf_op jit(solution)/shard_map/convert_element_type | solution.py:1172
  225.2 2.0 fusion.28
  227.3 2.6 fusion.29
  229.9 4.8 fusion.25
  235.5 1.3 copy-done.14
  236.8 2.8 multiply_reduce_fusion.7
  239.7 1.3 add_convert_fusion
  241.1 1.0 copy-done.53
  242.2 3.7 fusion.23
  246.9 9.0 %convolution_convert_fusion.1 = bf16[4096,1024]{1,0:T(8,128)(2,1)} fusion(bf16[320,4096]{1,0:T(8,128)(2,1)} %get-tuple-element.147, f32[320,1024]{1,0:T(8,128)S(1)} %copy-done.10, f32[1024]{0:T(1024)S(1)} %bitcast.193, f32[1024]{0:T(1024)S(1)} %bitcast.189, f32[320]{0:T(512)S(1)} %add_rsqrt_fusion, f32[320]{0:T(512)S(1)} %broadcast_multiply_fusion.4), kind=kOutput, calls=%fused_computation.7 | convolution fusion | flops 2690187264 | bytes 12331520 | tf_op jit(solution)/shard_map/sf,sd->fd/dot_general | solution.py:1126
  255.9 6.7 %convolution_convert_fusion = bf16[4096,1024]{1,0:T(8,128)(2,1)} fusion(bf16[320,4096]{1,0:T(8,128)(2,1)S(1)} %copy-done.54, bf16[320,1024]{1,0:T(8,128)(2,1)S(1)} %bitcast.138), kind=kOutput, calls=%fused_computation.6 | convolution fusion | flops 2688548864 | bytes 11665408 | tf_op jit(solution)/shard_map/sf,sd->fd/dot_general | solution.py:1126
  262.6 2.6 convolution_convert_fusion.3
  265.3 5.3 convolution_convert_fusion.2
  270.6 188.0 %shard_map.487 = (f32[4,128,1024]{2,1,0:T(8,128)}, f32[16,1024]{1,0:T(8,128)}) custom-call(bf16[4,2,2,2,96,1024]{5,4,3,2,1,0:T(8,128)(2,1)} %bitcast.164, bf16[4,2,2,2,32,1024]{5,4,3,2,1,0:T(8,128)(2,1)} %bitcast.158, bf16[4,2,2,2,128,1024]{5,4,3,2,1,0:T(8,128)(2,1)} %bitcast.156, bf16[4,2,2,2,128,1024]{5,4,3,2,1,0:T(8,128)(2,1)} %bitcast.157, ...), custom_call_target="tpu_custom_call" | custom-call | tf_op jit(solution)/shard_map/pallas_call | solution.py:728
  458.6 58.9 %shard_map.488 = (f32[1024,1024]{1,0:T(8,128)}, bf16[512,1024]{1,0:T(8,128)(2,1)}, bf16[512,1024]{1,0:T(8,128)(2,1)}, bf16[96,1024]{1,0:T(8,128)(2,1)}, bf16[32,...) custom-call(f32[4,128,1024]{2,1,0:T(8,128)} %get-tuple-element.62.re, ...), custom_call_target="tpu_custom_call" | custom-call | tf_op jit(solution)/shard_map/pallas_call | solution.py:908
  517.5 64.8 %shard_map.489 = bf16[512,1024]{1,0:T(8,128)(2,1)} custom-call(f32[1024,1024]{1,0:T(8,128)} %get-tuple-element.71.gram, bf16[512,1024]{1,0:T(8,128)(2,1)} %get-tuple-element.72.hi, bf16[512,1024]{1,0:T(8,128)(2,1)} %get-tuple-element.73.lo), custom_call_target="tpu_custom_call" | custom-call | flops 38999998464 | bytes 8000000 | tf_op jit(solution)/shard_map/pallas_call | solution.py:1056
  582.3 1.2 copy-done.2
  583.6 29.7 %shard_map.490 = (bf16[96,1024]{1,0:T(8,128)(2,1)S(1)}, bf16[32,1024]{1,0:T(8,128)(2,1)S(1)}, bf16[128,1024]{1,0:T(8,128)(2,1)S(1)}, bf16[128,1024]{1,0:T(8,128)(2,1)S(1)}) custom-call(bf16[4,128,1024]{2,1,0:T(8,128)(2,1)S(1)} %bitcast.141), custom_call_target="tpu_custom_call" | custom-call | tf_op jit(solution)/shard_map/pallas_call | solution.py:1106
  613.3 1.0 fusion.47
  614.3 1.0 fusion.48
  615.3 0.9 fusion.50
  616.8 1.2 convert.21
  618.1 1.2 convert.22
  619.3 1.1 multiply_add_fusion.1
  620.5 1.1 multiply_add_fusion.2
  621.6 1.0 multiply_add_fusion.3
  (165 shorter events, 7.1 us)
Async XLA Ops:
  0.7 3.5 copy-start.19
  0.7 3.5 copy-start.22
  0.7 3.5 copy-start.24
  0.7 3.6 copy-start.31
  0.7 3.6 copy-start.33
  0.7 3.6 copy-start.3
  0.8 3.6 copy-start.4
  4.3 151.7 %copy-start.44 = (f32[4,1024]{1,0:T(4,128)S(1)}, f32[4,1024]{1,0:T(4,128)}, u32[]{:S(2)}) copy-start(f32[4,1024]{1,0:T(4,128)} %param.37) | copy-start | bytes 49156
  4.3 151.7 %copy-start.49 = (f32[2,1024]{1,0:T(2,128)S(1)}, f32[2,1024]{1,0:T(2,128)}, u32[]{:S(2)}) copy-start(f32[2,1024]{1,0:T(2,128)} %param.36) | copy-start | bytes 24580
  4.4 152.9 %copy-start.50 = (f32[2,1024]{1,0:T(2,128)S(1)}, f32[2,1024]{1,0:T(2,128)}, u32[]{:S(2)}) copy-start(f32[2,1024]{1,0:T(2,128)} %param.34) | copy-start | bytes 24580
  149.0 3.3 copy-start.5
  152.2 3.2 copy-start.6
  164.2 4.6 copy-start.51
  181.8 14.4 %copy-start.9 = (f32[320,1024]{1,0:T(8,128)}, f32[320,1024]{1,0:T(8,128)S(1)}, u32[]{:S(2)}) copy-start(f32[320,1024]{1,0:T(8,128)S(1)} %get-tuple-element.140) | copy-start | bytes 3932164
  181.9 8.3 %slice-start.2 = ((s8[8388608]{0:T(1024)(128)(4,1)}), s8[4194304]{0:T(1024)(128)(4,1)S(1)}, s32[]{:S(2)}) async-start(s8[8388608]{0:T(1024)(128)(4,1)} %bitcast.144), calls=%async_computation.2 | async-start | bytes 8388608
  182.2 8.0 %slice-start.3 = ((s8[8388608]{0:T(1024)(128)(4,1)}), s8[4194304]{0:T(1024)(128)(4,1)S(1)}, s32[]{:S(2)}) async-start(s8[8388608]{0:T(1024)(128)(4,1)} %bitcast.144), calls=%async_computation.3 | async-start | bytes 8388608
  182.2 14.0 %slice-start.6 = ((s8[8388608]{0:T(1024)(128)(4,1)}), s8[4194304]{0:T(1024)(128)(4,1)S(1)}, s32[]{:S(2)}) async-start(s8[8388608]{0:T(1024)(128)(4,1)} %bitcast.151), calls=%async_computation.6 | async-start | bytes 8388608
  190.1 6.1 slice-start.7
  210.1 8.1 %copy-start.26 = (bf16[320,1024]{0,1:T(8,128)(2,1)}, bf16[320,1024]{0,1:T(8,128)(2,1)S(1)}, u32[]{:S(2)}) copy-start(bf16[320,1024]{0,1:T(8,128)(2,1)S(1)} %copy.73) | copy-start | bytes 1966084
  227.3 8.3 %slice-start = ((s8[6291456]{0:T(1024)(128)(4,1)}), s8[4194304]{0:T(1024)(128)(4,1)S(1)}, s32[]{:S(2)}) async-start(s8[6291456]{0:T(1024)(128)(4,1)} %bitcast.134), calls=%async_computation | async-start | bytes 8388608
  229.9 5.6 slice-start.1
  235.5 4.1 copy-start.7
  235.5 5.5 slice-start.4
  236.8 2.8 copy-start.12
  236.8 4.2 slice-start.5
  246.9 9.0 %copy-start.54 = (bf16[320,4096]{1,0:T(8,128)(2,1)S(1)}, bf16[320,4096]{1,0:T(8,128)(2,1)}, u32[]{:S(2)}) copy-start(bf16[320,4096]{1,0:T(8,128)(2,1)} %get-tuple-element.144) | copy-start | bytes 7864324
  255.9 6.7 %copy-start.13 = (f32[320,1024]{1,0:T(8,128)S(1)}, f32[320,1024]{1,0:T(8,128)}, u32[]{:S(2)}) copy-start(f32[320,1024]{1,0:T(8,128)} %copy-done.11) | copy-start | bytes 3932164
  255.9 6.7 %copy-start.16 = (bf16[16,64,320]{2,1,0:T(8,128)(2,1)S(1)}, bf16[16,64,320]{2,1,0:T(8,128)(2,1)}, u32[]{:S(2)}) copy-start(bf16[16,64,320]{2,1,0:T(8,128)(2,1)} %copy-done.15) | copy-start | bytes 1966084
  517.5 95.8 %copy-start.17 = (f32[128,1024]{1,0:T(8,128)S(1)}, f32[128,1024]{1,0:T(8,128)}, u32[]{:S(2)}) copy-start(f32[128,1024]{1,0:T(8,128)} %param.29) | copy-start | bytes 1572868
  583.6 30.7 %copy-start.18 = (f32[128,1024]{1,0:T(8,128)S(1)}, f32[128,1024]{1,0:T(8,128)}, u32[]{:S(2)}) copy-start(f32[128,1024]{1,0:T(8,128)} %param.28) | copy-start | bytes 1572868
  583.6 31.7 %copy-start.23 = (f32[96,1024]{1,0:T(8,128)S(1)}, f32[96,1024]{1,0:T(8,128)}, u32[]{:S(2)}) copy-start(f32[96,1024]{1,0:T(8,128)} %param.26) | copy-start | bytes 1179652
  613.3 3.5 copy-start.30
  614.3 3.7 copy-start.29
  616.1 3.1 copy-start.20
  616.1 3.1 copy-start.36
  618.1 3.5 copy-start.25
  618.1 3.5 copy-start.37
  619.3 3.2 copy-start.34
  619.3 3.2 copy-start.38
  619.3 3.9 copy-start.39
  619.3 3.9 copy-start.40
  619.3 3.9 copy-start.41
  620.4 3.5 copy-start.42
  620.4 3.5 copy-start.43
  620.4 4.1 copy-start.45
  620.4 4.1 copy-start.46
  620.4 4.1 copy-start.47
  620.4 4.1 copy-start.48
  (15 other events, 29.4 us)

commit v2 on v1

--- a/solution.py
+++ b/solution.py
@@ -411,27 +411,41 @@
     n = len(sizes)
     w = refs[:n]
     tok, cot = refs[n : n + 2]
-    mom = refs[n + 2 : 2 * n + 2]
-    full = refs[2 * n + 2 : 3 * n + 2]
-    tok_all, cot_all, mom_all = refs[3 * n + 2 : 3 * n + 5]
-    z_s, z_r, loc, t_s, t_r, m_s, m_r, p_s, p_r = refs[3 * n + 5 :]
+    full = refs[n + 2 : 2 * n + 2]
+    tok_all, cot_all = refs[2 * n + 2 : 2 * n + 4]
+    z_s, z_r, loc, t_s, t_r, p_s, p_r = refs[2 * n + 4 :]
     d, z, y, x, c = place()
     core, xn, yn, zn = partners(d, z, y, x, c)
     greet([core, xn, yn] + zn)
     held = []
+    inner = z * (3 - z) > 0
 
     def start(copy):
         copy.start()
         held.append(copy)
         return copy
 
-    def z_push(m):
-        for k in range(1, 4):
-            start(push(w[m], full[m].at[z, y, x, c], (z_s.at[m, k - 1], z_r.at[m, k - 1]), zn[k - 1]))
-
-    def z_wait(m, k):
-        slot = full[m].at[(z + 4 - k) % 4, y, x, c]
-        push(slot, slot, (z_s.at[m, k - 1], z_r.at[m, k - 1]), zn[k - 1]).wait_recv()
+    def source(j):
+        return (z, z + 1 - 2 * (z % 2), 2 - z // 2, 3 - 3 * (z // 2))[j]
+
+    def along(m, j, go):
+        slot = full[m].at[source(j), y, x, c]
+        if j == 0:
+
+            @pl.when(z < 3)
+            def _():
+                go(push(w[m], slot, (z_s.at[m, 0], z_r.at[m, z]), (d, z + 1)))
+
+            @pl.when(z > 0)
+            def _():
+                go(push(w[m], slot, (z_s.at[m, 1], z_r.at[m, z]), (d, z - 1)))
+
+        else:
+            beyond = 3 - z if j == 1 else 3 * (z - 1)
+
+            @pl.when(inner)
+            def _():
+                go(push(slot, slot, (z_s.at[m, 1 + j], z_r.at[m, source(j)]), (d, beyond)))
 
     locals_ = []
     for m in range(n):
@@ -442,51 +456,24 @@
         copy = pltpu.make_async_copy(a.at[z], b.at[z], loc.at[n + i])
         copy.start()
         locals_.append(copy)
-    z_push(0)
 
     def rows_push(i, a, b):
         for k in range(1, 4):
             start(push(a.at[(z + k) % 4], b.at[z], (t_s.at[i, k - 1], t_r.at[i, k - 1]), zn[k - 1]))
 
-    def mom_push():
-        for t in range(n):
-            here = mom_all.at[z, pl.ds(0, sizes[t])]
-
-            @pl.when(z == t)
-            def _(t=t, here=here):
-                pltpu.make_async_copy(mom[t], here, loc.at[n + 2]).start()
-
-            @pl.when(z != t)
-            def _(t=t, here=here):
-                push(mom[t], here, (m_s.at[t], m_r.at[z]), (d, t)).start()
-
-    def mom_wait():
-        for t in range(n):
-            here = mom_all.at[z, pl.ds(0, sizes[t])]
-
-            @pl.when(z == t)
-            def _(t=t, here=here):
-                pltpu.make_async_copy(mom[t], here, loc.at[n + 2]).wait()
-                for k in range(1, 4):
-                    s = (t + k) % 4
-                    there = mom_all.at[s, pl.ds(0, sizes[t])]
-                    push(mom[t], there, (m_s.at[t], m_r.at[s]), (d, s)).wait_recv()
-
-            @pl.when(z != t)
-            def _(t=t, here=here):
-                push(mom[t], here, (m_s.at[t], m_r.at[z]), (d, t)).wait_send()
-
     def sem(i, stage):
         return (p_s.at[stage, i], p_r.at[stage, i])
 
     def one(i):
         m, k = order[i]
         h = sizes[m] // 2
+        s = source(k)
         if k > 0:
-            z_wait(m, k)
+            slot = full[m].at[s, y, x, c]
+            push(slot, slot, (z_s.at[m, 1 + k], z_r.at[m, s]), core).wait_recv()
+            along(m, k, lambda copy: copy.start())
         else:
             locals_[m].wait()
-        s = (z + 4 - k) % 4
         a = full[m].at[s, y, x, c, pl.ds(0, h)]
         b = full[m].at[s, y, x, c, pl.ds(h, h)]
         start(push(a, a, sem(i, 0), xn))
@@ -495,7 +482,7 @@
     def two(i):
         m, k = order[i]
         h = sizes[m] // 2
-        s = (z + 4 - k) % 4
+        s = source(k)
         a = full[m].at[s, y, 1 - x, c, pl.ds(0, h)]
         push(a, a, sem(i, 0), xn).wait_recv()
         a = full[m].at[s, y, :, c, pl.ds(0, h)]
@@ -508,7 +495,7 @@
     def three(i):
         m, k = order[i]
         h = sizes[m] // 2
-        s = (z + 4 - k) % 4
+        s = source(k)
         a = full[m].at[s, 1 - y, :, c, pl.ds(0, h)]
         push(a, a, sem(i, 2), yn).wait_recv()
         b = full[m].at[s, :, 1 - x, c, pl.ds(h, h)]
@@ -517,63 +504,63 @@
         start(push(e, e, sem(i, 4), core))
 
     count = len(order)
+    go = lambda copy: copy.start()
+    along(0, 0, go)
+    along(1, 0, go)
     for i in range(count + 2):
         if i < count:
             one(i)
         if i == 0:
-            z_push(1)
             rows_push(0, tok, tok_all)
-            z_push(2)
-        if i == 5:
-            z_push(3)
+            along(2, 0, go)
+        if i == 4:
+            along(3, 0, go)
+        if i == 6:
             rows_push(1, cot, cot_all)
-            mom_push()
         if 1 <= i <= count:
             two(i - 1)
         if i >= 2:
             three(i - 2)
     for i in range(count):
         m, k = order[i]
-        e = full[m].at[(z + 4 - k) % 4, :, :, 1 - c]
+        e = full[m].at[source(k), :, :, 1 - c]
         push(e, e, sem(i, 4), core).wait_recv()
     for i, b in enumerate((tok_all, cot_all)):
         locals_[n + i].wait()
         for k in range(1, 4):
             slot = b.at[(z + 4 - k) % 4]
             push(slot, slot, (t_s.at[i, k - 1], t_r.at[i, k - 1]), zn[k - 1]).wait_recv()
-    mom_wait()
     for copy in held:
         copy.wait_send()
-
-
-def gather_all(weights, tok, cot, moms):
+    for m in range(n):
+        for j in range(4):
+            along(m, j, lambda copy: copy.wait_send())
+
+
+def gather_all(weights, tok, cot):
     sizes = tuple(v.shape[0] for v in weights)
     width = weights[0].shape[1]
-    order = [(0, 0), (1, 0), (2, 0), (0, 1), (0, 2), (0, 3), (1, 1), (1, 2), (1, 3)]
-    order += [(2, 1), (2, 2), (2, 3), (3, 0), (3, 1), (3, 2), (3, 3)]
+    order = [(m, 0) for m in range(4)] + [(m, k) for m in range(4) for k in (1, 2, 3)]
     count = len(order)
     anyspace = pl.BlockSpec(memory_space=pl.ANY)
     dma = pltpu.SemaphoreType.DMA
     return pl.pallas_call(
         functools.partial(gather_kernel, sizes, order),
         out_shape=[jax.ShapeDtypeStruct((4, 2, 2, 2, s, width), BF) for s in sizes]
-        + [jax.ShapeDtypeStruct(tok.shape, BF), jax.ShapeDtypeStruct(cot.shape, BF)]
-        + [jax.ShapeDtypeStruct((4, max(sizes), width), BF)],
-        in_specs=[anyspace] * (2 * len(sizes) + 2),
-        out_specs=[anyspace] * (len(sizes) + 3),
+        + [jax.ShapeDtypeStruct(tok.shape, BF), jax.ShapeDtypeStruct(cot.shape, BF)],
+        in_specs=[anyspace] * (len(sizes) + 2),
+        out_specs=[anyspace] * (len(sizes) + 2),
         scratch_shapes=[
-            dma((4, 3)),
-            dma((4, 3)),
-            dma((7,)),
+            dma((4, 5)),
+            dma((4, 4)),
+            dma((6,)),
             dma((2, 3)),
             dma((2, 3)),
-            dma((4,)),
-            dma((4,)),
             dma((5, count)),
             dma((5, count)),
         ],
         compiler_params=pltpu.CompilerParams(collective_id=1, has_side_effects=True, vmem_limit_bytes=8 << 20),
-    )(*weights, tok, cot, *moms)
+    )(*weights, tok, cot)
 
 
 def add_rows(dst, src, lead, rows):
@@ -588,20 +575,94 @@
     lax.fori_loop(0, lead * (rows // step), body, 0)
 
 
-def reduce_kernel(sizes, order, *refs):
-    n = len(sizes)
-    part = refs[:n]
-    small = refs[n]
-    total, small_out = refs[n + 1 : n + 3]
-    own = refs[n + 3 : 2 * n + 3]
-    got = refs[2 * n + 3 : 3 * n + 3]
-    mid = refs[3 * n + 3 : 4 * n + 3]
-    end = refs[4 * n + 3 : 5 * n + 3]
-    far, s_got, s_acc, s_z, loc, p_s, p_r, f_s, f_r, q_s, q_r = refs[5 * n + 3 :]
+PLANES = (1, 0, 2, 3)
+
+
+LINK = 93.5e3
+
+
+def plan(blocks, sizes, order, free_after, width):
+    todo = list(blocks)
+    done = []
+    events = []
+    link = {"x": 0.0, "y": 0.0, "z": 0.0}
+    now = 0.0
+    finished = set()
+
+    def carry(lane, start, rows):
+        begin = max(start, link[lane])
+        link[lane] = begin + rows * width * 2 * 2 / LINK
+        return link[lane] + 1.5
+
+    def emit(step):
+        nonlocal now
+        kind, i = step[0], step[1]
+        done.append(step)
+        finished.add(step)
+        s = sizes[order[i][0]]
+        if kind == "one":
+            now += s / 128 * 1.0
+            ready = max(carry("y", now, s), carry("x", now, s))
+            events.append((ready, ("two", i)))
+        elif kind == "two":
+            now += s / 128 * 0.6
+            ready = max(carry("x", now, s / 2), carry("y", now, s / 2))
+            events.append((ready, ("three", i)))
+        elif kind == "three":
+            now += s / 128 * 0.3
+            ready = carry("z", now, s)
+            events.append((ready, ("four", i)))
+            events.append((ready + 0.001, ("fourb", i)))
+        elif kind == "four":
+            finished.discard(step)
+            now += 0.2
+        elif kind == "fourb":
+            now += 0.2
+
+    while todo or events:
+        events.sort()
+        if events and events[0][0] <= now:
+            at, step = events.pop(0)
+            if step[0] == "fourb":
+                events.append((now + 3.0, ("fourc", step[1])))
+                events.sort()
+                continue
+            emit(step)
+            continue
+        if todo:
+            name, us, piece = todo[0]
+            blocked = piece is not None and piece >= free_after and ("one", piece - free_after) not in finished
+            if not blocked:
+                todo.pop(0)
+                done.append(("block", name))
+                now += us
+                if piece is not None:
+                    done.append(("push", piece))
+                    events.append((now + 3.0, ("one", piece)))
+                continue
+        now = max(now, events[0][0])
+    return done
+
+
+def backward_kernel(sizes, order, *refs):
+    n = 4
+    small_count = 16
+    (shrink, expand, outlet, intake, active, slope, middle, mixed, attended, second, first, x_in, cot) = refs[:13]
+    norm_gain, live = refs[13:15]
+    mom = refs[15:19]
+    total, small_out, mom_all, token_grad = refs[19:23]
+    refs = refs[23:]
+    own, mid, end, far = (refs[i * n : i * n + n] for i in range(4))
+    refs = refs[4 * n :]
+    (made, act, slo, wbuf, obuf, hgrad, wide, mgrad, branch, agrad) = refs[:10]
+    small, s_got, s_acc, s_z = refs[10:14]
+    loc, c_s, c_r, p_s, p_r, f_s, f_r, q_s, q_r, m_s, m_r, w_l = refs[14:]
     d, z, y, x, c = place()
     core, xn, yn, zn = partners(d, z, y, x, c)
     greet([core, xn, yn] + zn)
+    seq, width = cot.shape
     held = []
+    top = max(sizes)
 
     def start(copy):
         copy.start()
@@ -610,64 +671,93 @@
     def sem(i, stage):
         return (p_s.at[stage, i], p_r.at[stage, i])
 
-    def zero(i):
+    slots = made.shape[0]
+
+    def core_push(i):
         m, k = order[i]
-        start(push(part[m].at[k, :, :, 1 - c], got[m].at[k], sem(i, 0), core))
-        pltpu.make_async_copy(part[m].at[k, :, :, c], own[m].at[k], loc.at[i]).start()
+        return push(
+            made.at[i % slots, :, :, 1 - c, pl.ds(0, sizes[m])], own[m].at[k], (c_s.at[i], c_r.at[i]), core
+        )
 
     def one(i):
         m, k = order[i]
         s, h = sizes[m], sizes[m] // 2
-        pltpu.make_async_copy(part[m].at[k, :, :, c], own[m].at[k], loc.at[i]).wait()
-        push(part[m].at[k, :, :, 1 - c], got[m].at[k], sem(i, 0), core).wait_recv()
+        core_push(i).wait_recv()
         for j in range(2):
-            add_rows(own[m].at[k, j], got[m].at[k, j], 2, s)
-        start(push(own[m].at[k, 1 - y, :, pl.ds(0, h)], mid[m].at[k, 0], sem(i, 1), yn))
-        start(push(own[m].at[k, :, 1 - x, pl.ds(h, h)], mid[m].at[k, 1], sem(i, 2), xn))
+            for l in range(2):
+                add_rows(own[m].at[k, j, pl.ds(l, 1)], made.at[i % slots, j, l, pl.ds(c, 1)], 1, s)
+        start(push(own[m].at[k, 1 - y, :, pl.ds(0, h)], mid[m].at[k, 0], sem(i, 0), yn))
+        start(push(own[m].at[k, :, 1 - x, pl.ds(h, h)], mid[m].at[k, 1], sem(i, 1), xn))
 
     def two(i):
         m, k = order[i]
         h = sizes[m] // 2
-        push(mid[m].at[k, 0], mid[m].at[k, 0], sem(i, 1), yn).wait_recv()
+        push(mid[m].at[k, 0], mid[m].at[k, 0], sem(i, 0), yn).wait_recv()
         add_rows(own[m].at[k, y, :, pl.ds(0, h)], mid[m].at[k, 0], 2, h)
-        start(push(own[m].at[k, y, 1 - x, pl.ds(0, h)], end[m].at[k, pl.ds(0, h)], sem(i, 3), xn))
-        push(mid[m].at[k, 1], mid[m].at[k, 1], sem(i, 2), xn).wait_recv()
+        start(push(own[m].at[k, y, 1 - x, pl.ds(0, h)], end[m].at[k, pl.ds(0, h)], sem(i, 2), xn))
+        push(mid[m].at[k, 1], mid[m].at[k, 1], sem(i, 1), xn).wait_recv()
         add_rows(own[m].at[k, :, x, pl.ds(h, h)], mid[m].at[k, 1], 2, h)
-        start(push(own[m].at[k, 1 - y, x, pl.ds(h, h)], end[m].at[k, pl.ds(h, h)], sem(i, 4), yn))
+        start(push(own[m].at[k, 1 - y, x, pl.ds(h, h)], end[m].at[k, pl.ds(h, h)], sem(i, 3), yn))
+
+    def hop(i, p, go):
+        m, k = order[i]
+        side, to = (0, p + 1) if p < PLANES[m] else (1, p - 1)
+        at = side if PLANES[m] in (1, 2) else 0
+        go(push(own[m].at[k, y, x], far[m].at[at, k], (f_s.at[m, k], f_r.at[m, k, side]), (d, to)))
+
+    def came(m, k, side):
+        slot = far[m].at[side if PLANES[m] in (1, 2) else 0, k]
+        push(slot, slot, (f_s.at[m, k], f_r.at[m, k, side]), core).wait_recv()
 
     def three(i):
         m, k = order[i]
         s, h = sizes[m], sizes[m] // 2
-        push(end[m].at[k, pl.ds(0, h)], end[m].at[k, pl.ds(0, h)], sem(i, 3), xn).wait_recv()
-        push(end[m].at[k, pl.ds(h, h)], end[m].at[k, pl.ds(h, h)], sem(i, 4), yn).wait_recv()
+        push(end[m].at[k, pl.ds(0, h)], end[m].at[k, pl.ds(0, h)], sem(i, 2), xn).wait_recv()
+        push(end[m].at[k, pl.ds(h, h)], end[m].at[k, pl.ds(h, h)], sem(i, 3), yn).wait_recv()
         add_rows(own[m].at[k, pl.ds(y, 1), x], end[m].at[pl.ds(k, 1)], 1, s)
-
-        @pl.when(z != m)
+        for p in (0, 3):
+            if p != PLANES[m]:
+
+                @pl.when(z == p)
+                def _(p=p):
+                    hop(i, p, lambda copy: copy.start())
+
+    def four(i, far_hop):
+        m, k = order[i]
+        for p in (1, 2):
+            below = p < PLANES[m]
+            if p == PLANES[m] or far_hop != (p if below else 3 - p):
+                continue
+
+            @pl.when(z == p)
+            def _(p=p, below=below):
+                side = 0 if below else 1
+                came(m, k, side)
+                at = side if PLANES[m] in (1, 2) else 0
+                add_rows(own[m].at[k, pl.ds(y, 1), x], far[m].at[at, pl.ds(k, 1)], 1, sizes[m])
+                hop(i, p, lambda copy: copy.start())
+
+    def five(i):
+        m, k = order[i]
+        s, p = sizes[m], PLANES[m]
+        sides = [v for v in (0, 1) if p != 3 * v]
+
+        @pl.when(z == p)
         def _():
-            push(own[m].at[k, y, x], far.at[z, k, pl.ds(0, s)], (f_s.at[m, k], f_r.at[z, k]), (d, m)).start()
-
-    def four(i):
-        m, k = order[i]
-        s = sizes[m]
-
-        @pl.when(z == m)
-        def _():
-            for j in range(1, 4):
-                v = (m + j) % 4
-                slot = far.at[v, k, pl.ds(0, s)]
-                push(slot, slot, (f_s.at[m, k], f_r.at[v, k]), (d, v)).wait_recv()
+            for side in sides:
+                came(m, k, side)
 
             def body(r, carry):
                 at = pl.ds(pl.multiple_of(r * 16, 16), 16)
                 acc = own[m][k, y, x, at].astype(F32)
-                for j in range(1, 4):
-                    acc = acc + far[(m + j) % 4, k, at].astype(F32)
+                for side in range(len(sides)):
+                    acc = acc + far[m][side, k, at].astype(F32)
                 total[k, at] = acc
                 return carry
 
             lax.fori_loop(0, s // 16, body, 0)
             if s < total.shape[1]:
-                total[k, pl.ds(s, total.shape[1] - s)] = jnp.zeros((total.shape[1] - s, total.shape[2]), F32)
+                total[k, pl.ds(s, total.shape[1] - s)] = jnp.zeros((total.shape[1] - s, width), F32)
 
     def small_step(stage):
         to = (core, xn, yn)
@@ -684,71 +774,360 @@
             for k in range(1, 4):
                 start(push(s_acc.at[3], s_z.at[z], (q_s.at[2 + k], q_r.at[2 + k]), zn[k - 1]))
 
-    count = len(order)
-    lead = 4
-    for i in range(lead):
-        zero(i)
-    small_step(0)
-    for i in range(count + 4):
-        if i + lead < count:
-            zero(i + lead)
-        if i < count:
-            one(i)
-        if 1 <= i <= count:
-            two(i - 1)
-        if 2 <= i <= count + 1:
-            three(i - 2)
-        if 4 <= i:
-            four(i - 4)
-        if i in (2, 4, 6):
-            small_step(i // 2)
+    def moments(first):
+        for t in range(n):
+            p = PLANES[t]
+            here = mom_all.at[z, pl.ds(0, sizes[t])]
+
+            @pl.when(z == p)
+            def _(t=t, p=p, here=here):
+                copy = pltpu.make_async_copy(mom[t], here, loc.at[0])
+                if first:
+                    copy.start()
+                else:
+                    copy.wait()
+                    for k in range(1, 4):
+                        s = (p + k) % 4
+                        there = mom_all.at[s, pl.ds(0, sizes[t])]
+                        push(mom[t], there, (m_s.at[t], m_r.at[s]), (d, s)).wait_recv()
+
+            @pl.when(z != p)
+            def _(t=t, p=p, here=here):
+                copy = push(mom[t], here, (m_s.at[t], m_r.at[z]), (d, p))
+                if first:
+                    copy.start()
+                else:
+                    copy.wait_send()
+
+    unit = wbuf.shape[1]
+    count_units = shrink.shape[0] // unit
+
+    def load(u):
+        at = pl.ds(u * unit, unit)
+        return [
+            pltpu.make_async_copy(shrink.at[at], wbuf.at[u % 2], w_l.at[0, u % 2]),
+            pltpu.make_async_copy(expand.at[at], wbuf.at[2 + u % 2], w_l.at[1, u % 2]),
+            pltpu.make_async_copy(active.at[:, at], act.at[u % 2], w_l.at[2, u % 2]),
+            pltpu.make_async_copy(slope.at[:, at], slo.at[u % 2], w_l.at[3, u % 2]),
+        ]
+
+    def load_outlet():
+        return pltpu.make_async_copy(outlet, obuf, loc.at[1])
+
+    def load_intake(v):
+        return pltpu.make_async_copy(intake.at[pl.ds(v * unit, unit)], wbuf.at[v % 4], w_l.at[4, v % 4])
+
+    tdims = (((0,), (0,)), ((), ()))
+    ndims = (((1,), (1,)), ((), ()))
+
+    def mlp_one(u):
+        k, half = u // 2, u % 2
+        if u == 0:
+            for copy in load(0):
+                copy.start()
+        if u + 1 < count_units:
+            for copy in load(u + 1):
+                copy.start()
+        for copy in load(u):
+            copy.wait()
+        i = 2 * k
+
+        def body(j, carry):
+            cols = pl.ds(pl.multiple_of(j * 2 * top, 2 * top), 2 * top)
+            g = lax.dot_general(act[u % 2, :, cols], cot[...], tdims, preferred_element_type=F32)
+            made[i % slots, half, j] = g.astype(BF).reshape(2, top, width)
+            return carry
+
+        lax.fori_loop(0, unit // (2 * top), body, 0)
+
+        def grad(j, carry):
+            rows = pl.ds(pl.multiple_of(j * 256, 256), 256)
+            to = pl.ds(pl.multiple_of(j * 256 + half * unit, 256), 256)
+            g = lax.dot_general(cot[...], wbuf[u % 2, rows], ndims, preferred_element_type=F32)
+            hg = (g * slo[u % 2, :, rows]).astype(BF)
+            hgrad[:, to] = hg
+            small[pl.ds(2 + k, 1), to] = jnp.sum(hg.astype(F32), axis=0, keepdims=True)
+            return carry
+
+        lax.fori_loop(0, unit // 256, grad, 0)
+
+        def back(j, carry):
+            cols = pl.ds(pl.multiple_of(j * 256, 256), 256)
+            g = jnp.dot(hgrad[:, pl.ds(half * unit, unit)], wbuf[2 + u % 2, :, cols], preferred_element_type=F32)
+            if u == 0:
+                wide[:, cols] = g
+            else:
+                wide[:, cols] += g
+            return carry
+
+        lax.fori_loop(0, width // 256, back, 0)
+
+    def mlp_two(k):
+        i = 2 * k + 1
+
+        def body(j, carry):
+            cols = pl.ds(pl.multiple_of(j * 2 * top, 2 * top), 2 * top)
+            g = lax.dot_general(hgrad[:, cols], second[...], tdims, preferred_element_type=F32)
+            made[i % slots, j // 2, j % 2] = g.astype(BF).reshape(2, top, width)
+            return carry
+
+        lax.fori_loop(0, 4, body, 0)
+
+    chunk = 64
+
+    def norm_block(index, v_of, extra):
+        gain = norm_gain[pl.ds(index, 1)]
+
+        def body(i, carry):
+            at = pl.ds(pl.multiple_of(i * chunk, chunk), chunk)
+            v = v_of(at)
+            center = v - jnp.mean(v, axis=-1, keepdims=True)
+            r = lax.rsqrt(jnp.mean(center * center, axis=-1, keepdims=True) + norm_eps)
+            nrm = center * r
+            w = wide[at]
+            u = w * gain
+            down = r * (u - jnp.mean(u, axis=-1, keepdims=True) - nrm * jnp.mean(u * nrm, axis=-1, keepdims=True))
+            sums = extra(at, down)
+            new = [jnp.sum(w * nrm, axis=0, keepdims=True), jnp.sum(w, axis=0, keepdims=True)] + sums
+            return tuple(a + b for a, b in zip(carry, new))
+
+        zero = jnp.zeros((1, width), F32)
+        out = lax.fori_loop(0, seq // chunk, body, (zero,) * (4 if index else 2))
+        small[pl.ds(6 + index, 1)] = out[0]
+        small[pl.ds(8 + index, 1)] = out[1]
+        if index:
+            small[pl.ds(10, 1)] = out[2]
+            small[pl.ds(11, 1)] = out[3]
+
+    def second_norm_back():
+        load_outlet().start()
+        for v in range(4):
+            load_intake(v).start()
+
+        def extra(at, down):
+            g = cot[at].astype(F32)
+            m = g + down
+            mgrad[at] = m
+            low = m.astype(BF)
+            branch[at] = low
+            return [jnp.sum(low.astype(F32), axis=0, keepdims=True), jnp.sum(g, axis=0, keepdims=True)]
+
+        norm_block(1, lambda at: middle[at], extra)
+
+    def outlet_piece(k):
+        i = 8 + k
+        cols = pl.ds(k * 8 * sizes[1], 8 * sizes[1])
+        g = lax.dot_general(attended[:, cols], branch[...], tdims, preferred_element_type=F32)
+        made[i % slots, :, :, :, pl.ds(0, sizes[1])] = g.astype(BF).reshape(2, 2, 2, sizes[1], width)
+
+    def attended_back():
+        load_outlet().wait()
+
+        def body(j, carry):
+            rows = pl.ds(pl.multiple_of(j * 256, 256), 256)
+            g = lax.dot_general(branch[...], obuf[rows], ndims, preferred_element_type=F32)
+            agrad[:, rows] = g.astype(BF)
+            return carry
+
+        lax.fori_loop(0, width // 256, body, 0)
+
+    scale = HEAD_DIM ** (-0.5)
+
+    def heads(first_pair, pairs):
+        mask = live[...] > 0.0
+
+        def body(p, carry):
+            at = pl.ds(pl.multiple_of(p * 6 * HEAD_DIM, 6 * HEAD_DIM), 6 * HEAD_DIM)
+            both = mixed[:, at]
+            ag_both = agrad[:, pl.ds(pl.multiple_of(p * 2 * HEAD_DIM, 2 * HEAD_DIM), 2 * HEAD_DIM)]
+            parts, sums = [], []
+            for e in range(2):
+                q, k, v = (both[:, (3 * e + b) * HEAD_DIM : (3 * e + b + 1) * HEAD_DIM] for b in range(3))
+                ag = ag_both[:, e * HEAD_DIM : (e + 1) * HEAD_DIM]
+                s = lax.dot_general(q, k, ndims, preferred_element_type=F32) * scale
+                s = jnp.where(mask, s, masked_score)
+                s = jnp.exp(s - jnp.max(s, axis=-1, keepdims=True))
+                pr = s / jnp.sum(s, axis=-1, keepdims=True)
+                vg = lax.dot_general(pr.astype(BF), ag, tdims, preferred_element_type=F32)
+                dp = lax.dot_general(ag, v, ndims, preferred_element_type=F32)
+                ds = (pr * (dp - jnp.sum(dp * pr, axis=-1, keepdims=True))).astype(BF)
+                qg = jnp.dot(ds, k, preferred_element_type=F32) * scale
+                kg = lax.dot_general(ds, q, tdims, preferred_element_type=F32) * scale
+                parts += [qg.astype(BF), kg.astype(BF), vg.astype(BF)]
+                sums.append((jnp.sum(parts[-3].astype(F32), 0, keepdims=True), jnp.sum(parts[-1].astype(F32), 0, keepdims=True)))
+            mixed[:, at] = jnp.concatenate(parts, axis=1)
+            to = pl.ds(pl.multiple_of(p * 2 * HEAD_DIM, 2 * HEAD_DIM), 2 * HEAD_DIM)
+            small[pl.ds(0, 1), to] = jnp.concatenate([sums[0][0], sums[1][0]], axis=1)
+            small[pl.ds(1, 1), to] = jnp.concatenate([sums[0][1], sums[1][1]], axis=1)
+            return carry
+
+        lax.fori_loop(first_pair, first_pair + pairs, body, 0)
+
+    def intake_piece(k):
+        i = 12 + k
+        rows = 4 * sizes[0]
+
+        def body(j, carry):
+            cols = pl.ds(pl.multiple_of((2 * k + j) * rows, rows), rows)
+            g = lax.dot_general(mixed[:, cols], first[...], tdims, preferred_element_type=F32)
+            made[i % slots, j, :, :, pl.ds(0, sizes[0])] = g.astype(BF).reshape(2, 2, sizes[0], width)
+            return carry
+
+        lax.fori_loop(0, 2, body, 0)
+
+    def first_back(v):
+        load_intake(v).wait()
+
+        def body(j, carry):
+            cols = pl.ds(pl.multiple_of(j * 256, 256), 256)
+            g = jnp.dot(mixed[:, pl.ds(v * unit, unit)], wbuf[v % 4, :, cols], preferred_element_type=F32)
+            if v == 0:
+                wide[:, cols] = g
+            else:
+                wide[:, cols] += g
+            return carry
+
+        lax.fori_loop(0, width // 256, body, 0)
+        if v + 4 < intake.shape[0] // unit:
+            load_intake(v + 4).start()
+
+    def first_norm_back():
+        def extra(at, down):
+            token_grad[at] = (mgrad[at] + down).astype(BF)
+            return []
+
+        norm_block(0, lambda at: x_in[at].astype(F32), extra)
+
+    work = {}
+    blocks = []
+
+    def block(name, us, piece, fn):
+        work[name] = fn
+        blocks.append((name, us, piece))
+
+    for k in range(4):
+        block(("m", 2 * k), 3.0, None, functools.partial(mlp_one, 2 * k))
+        block(("m", 2 * k + 1), 3.0, 2 * k, functools.partial(mlp_one, 2 * k + 1))
+        block(("e", k), 1.5, 2 * k + 1, functools.partial(mlp_two, k))
+    block("n2", 3.0, None, second_norm_back)
+    for k in range(4):
+        block(("o", k), 0.5, 8 + k, functools.partial(outlet_piece, k))
+    block("ab", 1.5, None, attended_back)
+    for k in range(4):
+        block(("h", k), 7.0, None, functools.partial(heads, 2 * k, 2))
+        block(("i", k), 1.2, 12 + k, functools.partial(intake_piece, k))
+    for v in range(intake.shape[0] // unit):
+        block(("f", v), 0.8, None, functools.partial(first_back, v))
+    block("n1", 3.0, None, first_norm_back)
+    block("s0", 0.2, None, functools.partial(small_step, 0))
+
+    small[pl.ds(12, 4)] = jnp.zeros((4, width), F32)
+    moments(True)
+    steps = plan(blocks, sizes, order, slots, width)
+    pushed = {}
+    stage = 1
+    for step in steps:
+        kind = step[0]
+        if kind == "block":
+            name = step[1]
+            piece = {b[0]: b[2] for b in blocks}[name]
+            first_piece = piece if piece is not None else (2 * (name[1] // 2) if name[0] == "m" else None)
+            if first_piece is not None and first_piece - slots in pushed:
+                pushed.pop(first_piece - slots).wait_send()
+            work[name]()
+        elif kind == "push":
+            pushed[step[1]] = core_push(step[1])
+            pushed[step[1]].start()
+        elif kind == "one":
+            one(step[1])
+        elif kind == "two":
+            two(step[1])
+        elif kind == "three":
+            three(step[1])
+        elif kind == "four":
+            four(step[1], 1)
+        elif kind == "fourc":
+            four(step[1], 2)
+    for s in (1, 2, 3):
+        small_step(s)
+    for i in range(len(order)):
+        five(i)
     for k in range(1, 4):
         slot = s_z.at[(z + 4 - k) % 4]
         push(slot, slot, (q_s.at[2 + k], q_r.at[2 + k]), zn[k - 1]).wait_recv()
     small_out[...] = s_z[0] + s_z[1] + s_z[2] + s_z[3]
+    moments(False)
+    for copy in pushed.values():
+        copy.wait_send()
     for copy in held:
         copy.wait_send()
-    for m, k in order:
-
-        @pl.when(z != m)
-        def _(m=m, k=k):
-            slot = own[m].at[k, y, x]
-            push(slot, slot, (f_s.at[m, k], f_r.at[z, k]), (d, m)).wait_send()
-
-
-def reduce_all(parts, small):
-    sizes = tuple(v.shape[4] for v in parts)
-    width = parts[0].shape[5]
+    for i in range(len(order)):
+        for p in range(4):
+            if p != PLANES[order[i][0]]:
+
+                @pl.when(z == p)
+                def _(i=i, p=p):
+                    hop(i, p, lambda copy: copy.wait_send())
+
+
+def backward_all(weights, saved, norm_gain, live, moms, sizes):
+    intake, outlet, expand, shrink = weights
+    active, slope, middle, mixed, attended, second, first, x, cot = saved
+    seq, width = cot.shape
     top = max(sizes)
-    order = [(m, k) for m in (3, 2, 1, 0) for k in range(4)]
+    order = []
+    for k in range(4):
+        order += [(3, k), (2, k)]
+    order += [(1, k) for k in range(4)] + [(0, k) for k in range(4)]
     count = len(order)
     anyspace = pl.BlockSpec(memory_space=pl.ANY)
     vmem = pl.BlockSpec(memory_space=pltpu.VMEM)
     dma = pltpu.SemaphoreType.DMA
+    unit = 512
     return pl.pallas_call(
-        functools.partial(reduce_kernel, sizes, order),
-        out_shape=[jax.ShapeDtypeStruct((4, top, width), F32), jax.ShapeDtypeStruct(small.shape, F32)],
-        in_specs=[anyspace] * len(sizes) + [vmem],
-        out_specs=[vmem, vmem],
+        functools.partial(backward_kernel, sizes, order),
+        out_shape=[
+            jax.ShapeDtypeStruct((4, top, width), F32),
+            jax.ShapeDtypeStruct((16, width), F32),
+            jax.ShapeDtypeStruct((4, top, width), BF),
+            jax.ShapeDtypeStruct((seq, width), BF),
+        ],
+        in_specs=[anyspace] * 6 + [vmem] * 9 + [anyspace] * 4,
+        out_specs=[vmem, vmem, anyspace, vmem],
         scratch_shapes=[pltpu.VMEM((4, 2, 2, s, width), BF) for s in sizes]
-        + [pltpu.VMEM((4, 2, 2, s, width), BF) for s in sizes]
         + [pltpu.VMEM((4, 2, 2, s // 2, width), BF) for s in sizes]
         + [pltpu.VMEM((4, s, width), BF) for s in sizes]
+        + [pltpu.VMEM((2 if p in (1, 2) else 1, 4, s, width), BF) for s, p in zip(sizes, PLANES)]
         + [
-            pltpu.VMEM((4, 4, top, width), BF),
-            pltpu.VMEM((3,) + small.shape, F32),
-            pltpu.VMEM((4,) + small.shape, F32),
-            pltpu.VMEM((4,) + small.shape, F32),
+            pltpu.VMEM((3, 2, 2, 2, top, width), BF),
+            pltpu.VMEM((2, seq, unit), BF),
+            pltpu.VMEM((2, seq, unit), F32),
+            pltpu.VMEM((4, unit, width), BF),
+            pltpu.VMEM((width, width), BF),
+            pltpu.VMEM((seq, width), BF),
+            pltpu.VMEM((seq, width), F32),
+            pltpu.VMEM((seq, width), F32),
+            pltpu.VMEM((seq, width), BF),
+            pltpu.VMEM((seq, width), BF),
+            pltpu.VMEM((16, width), F32),
+            pltpu.VMEM((3, 16, width), F32),
+            pltpu.VMEM((4, 16, width), F32),
+            pltpu.VMEM((4, 16, width), F32),
+            dma((2,)),
             dma((count,)),
-            dma((5, count)),
-            dma((5, count)),
+            dma((count,)),
+            dma((4, count)),
+            dma((4, count)),
             dma((4, 4)),
-            dma((4, 4)),
+            dma((4, 4, 2)),
             dma((6,)),
             dma((6,)),
+            dma((4,)),
+            dma((4,)),
+            dma((5, 4)),
         ],
         compiler_params=pltpu.CompilerParams(collective_id=2, has_side_effects=True, vmem_limit_bytes=VMEM_LIMIT),
-    )(*parts, small)
+    )(shrink, expand, outlet, intake, active, slope, middle, mixed, attended, second, first, x, cot, norm_gain, live, *moms)
 
 
 def gram_kernel(sizes, *refs):
@@ -776,16 +1155,19 @@
 
     lax.fori_loop(0, 4 * (top // 16), cast, 0)
     for t in range(n):
-
-        @pl.when(z == t)
-        def _(t=t):
+        p = PLANES[t]
+
+        @pl.when(z == p)
+        def _(t=t, p=p):
             s = sizes[t]
             for k in range(1, 4):
-                v = (t + k) % 4
+                v = (p + k) % 4
                 push(low_g.at[v, pl.ds(0, s)], grads[t], (g_s.at[v], g_r.at[t]), (d, v)).start()
-            pltpu.make_async_copy(low_g.at[t, pl.ds(0, s)], grads[t], loc.at[0]).start()
-
-    height = jnp.where(z == 0, sizes[0], jnp.where(z == 1, sizes[1], jnp.where(z == 2, sizes[2], sizes[3])))
+            pltpu.make_async_copy(low_g.at[p, pl.ds(0, s)], grads[t], loc.at[0]).start()
+
+    height = 0
+    for t in range(n):
+        height = jnp.where(z == PLANES[t], sizes[t], height)
 
     def make(i, carry):
         k, r = i // (top // 16), (i % (top // 16)) * 16
@@ -884,16 +1266,16 @@
             slot = b.at[(z + 4 - k) % 4]
             push(slot, slot, (o_s.at[i, k - 1], o_r.at[i, k - 1]), zn[k - 1]).wait_recv()
     for t in range(n):
-        s = sizes[t]
-
-        @pl.when(z == t)
-        def _(t=t, s=s):
-            pltpu.make_async_copy(low_g.at[t, pl.ds(0, s)], grads[t], loc.at[0]).wait()
+        s, p = sizes[t], PLANES[t]
+
+        @pl.when(z == p)
+        def _(t=t, s=s, p=p):
+            pltpu.make_async_copy(low_g.at[p, pl.ds(0, s)], grads[t], loc.at[0]).wait()
             for k in range(1, 4):
-                v = (t + k) % 4
+                v = (p + k) % 4
                 push(low_g.at[v, pl.ds(0, s)], grads[t], (g_s.at[v], g_r.at[t]), (d, v)).wait_send()
 
-        @pl.when(z != t)
+        @pl.when(z != p)
         def _(t=t):
             push(grads[t], grads[t], (g_s.at[t], g_r.at[t]), (d, t)).wait_recv()
     for copy in held:
@@ -1076,26 +1458,26 @@
     core, xn, yn, zn = partners(d, z, y, x, c)
     greet(zn)
     for t in range(n):
-        s = sizes[t]
-
-        @pl.when(z == t)
-        def _(t=t, s=s):
+        s, p = sizes[t], PLANES[t]
+
+        @pl.when(z == p)
+        def _(t=t, s=s, p=p):
             for k in range(1, 4):
-                v = (t + k) % 4
+                v = (p + k) % 4
                 push(done.at[v, pl.ds(0, s)], rows[t], (s_s.at[v], s_r.at[t]), (d, v)).start()
-            pltpu.make_async_copy(done.at[t, pl.ds(0, s)], rows[t], loc.at[0]).start()
+            pltpu.make_async_copy(done.at[p, pl.ds(0, s)], rows[t], loc.at[0]).start()
 
     for t in range(n):
-        s = sizes[t]
-
-        @pl.when(z == t)
-        def _(t=t, s=s):
-            pltpu.make_async_copy(done.at[t, pl.ds(0, s)], rows[t], loc.at[0]).wait()
+        s, p = sizes[t], PLANES[t]
+
+        @pl.when(z == p)
+        def _(t=t, s=s, p=p):
+            pltpu.make_async_copy(done.at[p, pl.ds(0, s)], rows[t], loc.at[0]).wait()
             for k in range(1, 4):
-                v = (t + k) % 4
+                v = (p + k) % 4
                 push(done.at[v, pl.ds(0, s)], rows[t], (s_s.at[v], s_r.at[t]), (d, v)).wait_send()
 
-        @pl.when(z != t)
+        @pl.when(z != p)
         def _(t=t):
             push(rows[t], rows[t], (s_s.at[t], s_r.at[t]), (d, t)).wait_recv()
 
@@ -1130,11 +1512,6 @@
         r = lax.rsqrt(jnp.mean(center * center, axis=-1, keepdims=True) + norm_eps)
         n = center * r
         return n * g + s, n, r
-
-    def norm_back(n, r, g, w):
-        u = w * g
-        down = r * (u - jnp.mean(u, axis=-1, keepdims=True) - n * jnp.mean(u * n, axis=-1, keepdims=True))
-        return down, jnp.sum(w * n, axis=0), jnp.sum(w, axis=0)
 
     rows = x.astype(F32)
     first, n1, r1 = norm(rows, norm_gain[0], model_bias[0])
@@ -1153,47 +1530,8 @@
     bell = 0.5 * (1.0 + lax.erf(hidden * (0.5**0.5)))
     active = (hidden * bell).astype(BF)
     output = middle + ein("sf,fd->sd", active, shrink) + model_bias[3]
-    shrink_grad = ein("sf,sd->fd", active, cot)
-    active_grad = ein("sd,fd->sf", cot, shrink)
     slope = bell + hidden * jnp.exp(-0.5 * hidden * hidden) * (0.5 / jnp.pi) ** 0.5
-    hidden_grad = (active_grad * slope).astype(BF)
-    hidden_bias_grad = jnp.sum(hidden_grad.astype(F32), axis=0)
-    expand_grad = ein("sf,sd->fd", hidden_grad, second)
-    second_grad = ein("sf,fd->sd", hidden_grad, expand)
-    down, gain_two, shift_two = norm_back(n2, r2, norm_gain[1], second_grad)
-    cot_float = cot.astype(F32)
-    middle_grad = cot_float + down
-    branch = middle_grad.astype(BF)
-    outlet_grad = ein("sc,sd->cd", attended, branch)
-    attended_grad = ein("sd,cd->sc", branch, outlet).astype(BF).reshape(seq, heads, HEAD_DIM)
-    values_grad = ein("hqk,qhe->khe", attention16, attended_grad)
-    attention_grad = ein("qhe,khe->hqk", attended_grad, v)
-    score_grad = attention * (attention_grad - jnp.sum(attention_grad * attention, axis=-1, keepdims=True))
-    score_grad = score_grad.astype(BF)
-    queries_grad = ein("hqk,khe->qhe", score_grad, k) * scale
-    keys_grad = ein("hqk,qhe->khe", score_grad, q) * scale
-    mixed_grad = jnp.stack([queries_grad, keys_grad, values_grad], axis=2).astype(BF)
-    sums = jnp.sum(mixed_grad.astype(F32), axis=0)
-    mixed_grad = mixed_grad.reshape(seq, 3 * width)
-    intake_grad = ein("sr,sd->rd", mixed_grad, first)
-    first_grad = ein("sr,rd->sd", mixed_grad, intake)
-    down, gain_one, shift_one = norm_back(n1, r1, norm_gain[0], first_grad)
-    token_grad = middle_grad + down
-    small = jnp.concatenate(
-        [
-            sums[:, 0].reshape(1, width),
-            sums[:, 2].reshape(1, width),
-            hidden_bias_grad.reshape(-1, width),
-            gain_one[None],
-            gain_two[None],
-            shift_one[None],
-            shift_two[None],
-            jnp.sum(branch.astype(F32), axis=0)[None],
-            jnp.sum(cot_float, axis=0)[None],
-        ]
-    )
-    grads = tuple(g.astype(BF) for g in (intake_grad, outlet_grad, expand_grad, shrink_grad))
-    return output.astype(BF), token_grad.astype(BF), grads, small
+    return output.astype(BF), (active, slope, middle, mixed.reshape(seq, 3 * width), attended, second, first, x, cot)
 
 
 def per_device_fast(
@@ -1231,21 +1569,16 @@
         [v.astype(BF) for v in masters],
         tokens.reshape(-1, local, width),
         cotangent.reshape(-1, local, width),
-        [v.astype(BF) for v in moments],
     )
     whole = [v.reshape(-1, width) for v in gathered[:4]]
     x, cot = (v.reshape(-1, width) for v in gathered[4:6])
     seq = x.shape[0]
     keep = lax.dynamic_index_in_dim(keep_mask.reshape(-1, seq), z, 0, keepdims=False)
     live = jnp.logical_or(keep != 0, jnp.arange(seq) < BUF)
-    out, token_grad, grads, small = whole_image(
-        x, cot, live, whole, head_bias, expand_bias, norm_gain, model_bias
-    )
-    count = small.shape[0]
-    small = jnp.pad(small, ((0, -count % 8), (0, 0)))
-    parts = [g.reshape(4, 2, 2, 2, s, width) for g, s in zip(grads, sizes)]
-    total, small = reduce_all(parts, small)
-    made = gram_all(total, gathered[6], out.reshape(-1, local, width), token_grad.reshape(-1, local, width), sizes)
+    out, saved = whole_image(x, cot, live, whole, head_bias, expand_bias, norm_gain, model_bias)
+    moms = [v.astype(BF) for v in moments]
+    total, small, mom, token_grad = backward_all(whole, saved, norm_gain, live.astype(F32)[None], moms, sizes)
+    made = gram_all(total, mom, out.reshape(-1, local, width), token_grad.reshape(-1, local, width), sizes)
     gram, hi, lo = made[:3]
     shards = [g.astype(F32) for g in made[3:7]]
     output = made[7].reshape(shape).astype(F32)

time: 630 us -> 507 us (0.80)
  Pallas kernels: 482 us -> 417 us
  matrix products: 88.9 us -> 29.2 us
    dot_general x17 -> x6, matrix products: 81.2 us -> 29.2 us  [ein(): return jnp.einsum(form, a, b, preferred_element_type=F32)]
    pallas_call x1, Pallas kernels: 188 us -> 151 us  [backward_all(): pl.pallas_call(functools.partial(backward_kernel, sizes, order), out_shap...]
    pallas_call x1, Pallas kernels: 141 us -> 115 us  [gather_all(): pl.pallas_call(functools.partial(gather_kernel, sizes, order), out_shape=...]
    sub x0 -> x1, other arithmetic: none -> 8.49 us  [softmax_rows(): powers = jnp.exp(scores - largest)]
    sub x1 -> x0, matrix products: 7.71 us -> none  [softmax_rows(): powers = jnp.exp(scores - largest)]
    unnamed x126 -> x100, local copies, waits for them, and re-layouts: 15.2 us -> 11.4 us
where the time goes in v2:
time: 507 us; the launch traced here: 498 us
  Pallas kernels  417 us (82%)
  other arithmetic  31.5 us (6%)
  matrix products  29.2 us (6%)
  local copies, waits for them, and re-layouts  19 us (4%)
    pallas_call x1, Pallas kernels, backward_all(): pl.pallas_call(functools.partial(backward_kernel, sizes, order), out_shap...  151 us
    pallas_call x1, Pallas kernels, gather_all(): pl.pallas_call(functools.partial(gather_kernel, sizes, order), out_shape=...  115 us
    pallas_call x1, Pallas kernels, polish(): pl.pallas_call(polish_kernel, out_shape=jax.ShapeDtypeStruct((rows, width...  64.8 us
    pallas_call x1, Pallas kernels, gram_all(): pl.pallas_call(functools.partial(gram_kernel, sizes), out_shape=[jax.Shap...  60.6 us
    dot_general x6, matrix products, ein(): return jnp.einsum(form, a, b, preferred_element_type=F32)  29.2 us
    pallas_call x1, Pallas kernels, return_all(): pl.pallas_call(functools.partial(return_kernel, sizes), out_shape=[jax.Sh...  26 us
    unnamed x100, local copies, waits for them, and re-layouts  11.4 us

profile of v2, /device:TPU:8, one launch (start us, length us, event | category | flops | bytes accessed | tf_op | source)
XLA Modules:
  0.0 498.0 jit_solution(8151511995758682424)
XLA Ops:
  0.7 1.1 convert_element_type.113.refs_0_
  1.8 0.9 convert_element_type.114.refs_1_
  2.8 1.1 convert_element_type.115.refs_2_
  3.8 1.1 convert_element_type.116.refs_3_
  4.9 114.8 %shard_map.486 = (bf16[4,2,2,2,96,1024]{5,4,3,2,1,0:T(8,128)(2,1)S(1)}, bf16[4,2,2,2,32,1024]{5,4,3,2,1,0:T(8,128)(2,1)S(1)}, bf16[4,2,2,2,128,1024]{5,4,3,2,1,0...) custom-call(bf16[96,1024]{1,0:T(8,128)(2,1)S(1)} %convert_element_ty, ...), custom_call_target="tpu_custom_call" | custom-call | tf_op jit(solution)/shard_map/pallas_call | solution.py:547
  119.7 3.3 copy-done.1
  123.0 3.2 copy-done.2
  126.2 2.7 copy-done.4
  128.9 0.8 copy-done.8
  129.7 0.7 fusion.41
  130.6 0.3 fusion.17
  130.9 0.7 rsqrt.22
  131.6 0.7 div.64
  132.3 0.3 fusion.20
  133.0 6.3 %fusion.6.refs_7_ = bf16[320,3072]{1,0:T(8,128)(2,1)} fusion(bf16[320,1024]{1,0:T(8,128)(2,1)S(1)} %bitcast.80, bf16[3072,1024]{1,0:T(8,128)(2,1)} %bitcast.68, f32[3072]{0:T(1024)S(1)} %add.158), kind=kOutput, calls=%fused_computation.14 | convolution fusion | flops 2015232000 | bytes 8925184 | tf_op jit(solution)/shard_map/sd,rd->sr/dot_general | solution.py:1508
  139.3 4.1 copy.64
  143.4 5.7 %fusion.25 = f32[16,320,320]{1,2,0:T(8,128)} fusion(bf16[320,16,3,64]{0,3,2,1:T(8,128)(2,1)} %bitcast.74), kind=kOutput, calls=%fused_computation.41 | convolution fusion | flops 209715200 | bytes 8126464 | tf_op jit(solution)/shard_map/qhe,khe->hqk/dot_general | solution.py:1508
  149.1 0.6 or_convert_fusion
  149.7 8.5 %fusion.43 = (f32[16,320]{1,0:T(8,128)S(1)}, f32[16,320,320]{1,2,0:T(8,128)S(1)}) fusion(f32[16,320,320]{1,2,0:T(8,128)} %fusion.25, pred[320]{0:T(512)(128)(4,1)S(1)} %fusion.30), kind=kOutput, calls=%fused_computation.89 | output fusion | flops 9830719 | bytes 13128000 | tf_op jit(solution)/shard_map/sub | solution.py:42
  158.2 2.2 fusion.14
  160.5 1.0 fusion.44
  161.5 0.3 multiply_reduce_fusion
  161.8 1.3 fusion.24
  163.2 6.9 %fusion.5 = (f32[320,4096]{1,0:T(8,128)}, bf16[320,4096]{1,0:T(8,128)(2,1)}) fusion(f32[4096]{0:T(1024)S(1)} %copy-done.47, bf16[320,1024]{1,0:T(8,128)(2,1)S(1)} %get-tuple-element.134.refs_9_, bf16[4096,1024]{1,0:T(8,128)(2,1)S(1)} %bitcast.65), kind=kOutput, calls=%fused_computation.10 | convolution fusion | flops 2698772480 | bytes 16924672 | tf_op jit(solution)/shard_map/sd,fd->sf/dot_general | solution.py:1508
  170.1 1.1 copy.69.refs_8_
  171.3 0.7 convert_element_type.130.refs_15_
  172.0 0.6 convert_element_type.131.refs_16_
  172.6 0.7 convert_element_type.132.refs_17_
  173.4 0.7 convert_element_type.133.refs_18_
  174.1 150.6 %shard_map.487 = (f32[4,128,1024]{2,1,0:T(8,128)}, f32[16,1024]{1,0:T(8,128)}, bf16[4,128,1024]{2,1,0:T(8,128)(2,1)}, bf16[320,1024]{1,0:T(8,128)(2,1)}) custom-call(bf16[4096,1024]{1,0:T(8,128)(2,1)} %bitcast.60, bf16[4096,1024]{1,0:T(8,128)(2,1)} %bitcast.62, bf16[1024,1024]{1,0:T(8,128)(2,1)} %bitcast.67, bf16[3072,1024]{1,0:T(8,128)(2,1)} %bitcast.69, ...), custom_call_target="tpu_custom_call" | custom-call | tf_op jit(solution)/shard_map/pallas_call | solution.py:1087
  324.7 7.1 %fusion.16 = bf16[320,1024]{1,0:T(8,128)(2,1)} fusion(f32[320,1024]{1,0:T(8,128)S(1)} %copy-done.10, bf16[320,4096]{1,0:T(8,128)(2,1)S(1)} %copy-done.11, bf16[4096,1024]{1,0:T(8,128)(2,1)} %bitcast.61, f32[1024]{0:T(1024)S(1)} %bitcast.92), kind=kOutput, calls=%fused_computation.29 | convolution fusion | flops 2685337600 | bytes 12980224 | tf_op jit(solution)/shard_map/sf,fd->sd/dot_general | solution.py:1508
  331.8 60.6 %shard_map.488 = (f32[1024,1024]{1,0:T(8,128)}, bf16[512,1024]{1,0:T(8,128)(2,1)}, bf16[512,1024]{1,0:T(8,128)(2,1)}, bf16[96,1024]{1,0:T(8,128)(2,1)}, bf16[32,...) custom-call(f32[4,128,1024]{2,1,0:T(8,128)} %get-tuple-element.63.re, ...), custom_call_target="tpu_custom_call" | custom-call | tf_op jit(solution)/shard_map/pallas_call | solution.py:1290
  392.5 2.4 convert.2
  394.9 1.2 convert.3
  396.1 1.0 multiply_add_fusion.2
  397.2 0.7 multiply_add_fusion.3
  397.9 1.1 multiply_add_fusion.1
  399.0 1.1 multiply_add_fusion
  400.1 0.7 add_divide_fusion.2
  400.8 0.6 add_divide_fusion
  401.4 0.6 add_divide_fusion.1
  402.1 64.8 %shard_map.489 = bf16[512,1024]{1,0:T(8,128)(2,1)} custom-call(f32[1024,1024]{1,0:T(8,128)} %get-tuple-element.73.gram, bf16[512,1024]{1,0:T(8,128)(2,1)} %get-tuple-element.74.hi, bf16[512,1024]{1,0:T(8,128)(2,1)} %get-tuple-element.75.lo), custom_call_target="tpu_custom_call" | custom-call | flops 38999998464 | bytes 8000000 | tf_op jit(solution)/shard_map/pallas_call | solution.py:1438
  466.9 1.2 copy-done.5
  468.1 26.0 %shard_map.490 = (bf16[96,1024]{1,0:T(8,128)(2,1)S(1)}, bf16[32,1024]{1,0:T(8,128)(2,1)S(1)}, bf16[128,1024]{1,0:T(8,128)(2,1)S(1)}, bf16[128,1024]{1,0:T(8,128)(2,1)S(1)}) custom-call(bf16[4,128,1024]{2,1,0:T(8,128)(2,1)S(1)} %bitcast.70), custom_call_target="tpu_custom_call" | custom-call | tf_op jit(solution)/shard_map/pallas_call | solution.py:1488
  494.1 0.9 fusion.40
  495.0 0.7 fusion.39
  495.7 1.0 fusion.38
  496.6 1.0 fusion.37
  (110 shorter events, 0.9 us)
Async XLA Ops:
  0.7 4.2 copy-start.6
  0.7 4.2 copy-start.7
  0.7 129.0 %copy-start.37 = (f32[4,1024]{1,0:T(4,128)S(1)}, f32[4,1024]{1,0:T(4,128)}, u32[]{:S(2)}) copy-start(f32[4,1024]{1,0:T(4,128)} %param.37) | copy-start | bytes 49156
  0.7 129.7 %copy-start.31 = (f32[2,1024]{1,0:T(2,128)S(1)}, f32[2,1024]{1,0:T(2,128)}, u32[]{:S(2)}) copy-start(f32[2,1024]{1,0:T(2,128)} %refs_13_.1) | copy-start | bytes 24580
  4.9 127.7 %copy-start.44 = (f32[2,1024]{1,0:T(2,128)S(1)}, f32[2,1024]{1,0:T(2,128)}, u32[]{:S(2)}) copy-start(f32[2,1024]{1,0:T(2,128)} %param.34) | copy-start | bytes 24580
  119.7 3.3 copy-start.1
  123.0 3.2 copy-start.2
  126.2 2.7 copy-start.4
  129.7 30.7 %copy-start.3 = (bf16[4,2,2,2,32,1024]{5,4,3,2,1,0:T(8,128)(2,1)}, bf16[4,2,2,2,32,1024]{5,4,3,2,1,0:T(8,128)(2,1)S(1)}, u32[]{:S(2)}) copy-start(bf16[4,2,2,2,32,1024]{5,4,3,2,1,0:T(8,128)(2,1)S(1)} %get-tuple-element.59) | copy-start | bytes 6291460
  129.7 32.0 %copy-start = (bf16[4,80,1024]{2,1,0:T(8,128)(2,1)}, bf16[4,80,1024]{2,1,0:T(8,128)(2,1)S(1)}, u32[]{:S(2)}) copy-start(bf16[4,80,1024]{2,1,0:T(8,128)(2,1)S(1)} %get-tuple-element.61) | copy-start | bytes 1966084
  143.4 5.7 %copy-start.45 = (s32[2,2,320]{2,1,0:T(2,128)S(1)}, s32[2,2,320]{2,1,0:T(2,128)}, u32[]{:S(2)}) copy-start(s32[2,2,320]{2,1,0:T(2,128)} %param.25) | copy-start | bytes 15364
  158.2 4.9 slice-start
  158.2 4.9 slice-start.1
  160.4 1.3 copy-start.32
  160.4 1.3 copy-start.38
  160.5 1.3 copy-start.39
  161.4 1.7 copy-start.9
  161.4 1.7 copy-start.47
  163.1 7.0 %copy-start.12 = (bf16[320,1024]{1,0:T(8,128)(2,1)}, bf16[320,1024]{1,0:T(8,128)(2,1)S(1)}, u32[]{:S(2)}) copy-start(bf16[320,1024]{1,0:T(8,128)(2,1)S(1)} %get-tuple-element.134.refs_9_) | copy-start | bytes 1966084
  163.2 8.1 %copy-start.19 = (f32[96,1024]{1,0:T(8,128)S(1)}, f32[96,1024]{1,0:T(8,128)}, u32[]{:S(2)}) copy-start(f32[96,1024]{1,0:T(8,128)} %param.30) | copy-start | bytes 1179652
  163.2 8.8 %copy-start.23 = (f32[32,1024]{1,0:T(8,128)S(1)}, f32[32,1024]{1,0:T(8,128)}, u32[]{:S(2)}) copy-start(f32[32,1024]{1,0:T(8,128)} %param.31) | copy-start | bytes 393220
  170.1 2.5 copy-start.13
  170.1 3.2 copy-start.15
  174.1 150.6 %copy-start.10 = (f32[320,1024]{1,0:T(8,128)S(1)}, f32[320,1024]{1,0:T(8,128)}, u32[]{:S(2)}) copy-start(f32[320,1024]{1,0:T(8,128)} %copy-done.9) | copy-start | bytes 3932164
  174.1 150.6 %copy-start.11 = (bf16[320,4096]{1,0:T(8,128)(2,1)S(1)}, bf16[320,4096]{1,0:T(8,128)(2,1)}, u32[]{:S(2)}) copy-start(bf16[320,4096]{1,0:T(8,128)(2,1)} %get-tuple-element.115.refs_4_) | copy-start | bytes 7864324
  174.1 150.6 %copy-start.46 = (f32[1,1024]{1,0:T(1,128)S(1)}, f32[1,1024]{1,0:T(1,128)}, u32[]{:S(2)}) copy-start(f32[1,1024]{1,0:T(1,128)} %get-tuple-element.121) | copy-start | bytes 12292
  392.4 2.5 copy-start.22
  392.4 3.7 copy-start.20
  392.5 3.7 copy-start.28
  392.5 4.7 copy-start.24
  392.5 4.7 copy-start.29
  394.9 3.0 copy-start.14
  394.9 3.0 copy-start.27
  394.9 4.1 copy-start.16
  394.9 4.1 copy-start.26
  397.1 3.0 copy-start.30
  397.1 3.0 copy-start.40
  397.1 3.0 copy-start.41
  397.1 3.0 copy-start.42
  397.1 3.0 copy-start.43
  397.1 3.7 copy-start.33
  397.1 3.7 copy-start.34
  397.1 4.3 copy-start.35
  397.1 4.3 copy-start.36
  402.1 92.0 %copy-start.21 = (f32[96,1024]{1,0:T(8,128)S(1)}, f32[96,1024]{1,0:T(8,128)}, u32[]{:S(2)}) copy-start(f32[96,1024]{1,0:T(8,128)} %param.26) | copy-start | bytes 1179652
  402.1 92.9 %copy-start.25 = (f32[32,1024]{1,0:T(8,128)S(1)}, f32[32,1024]{1,0:T(8,128)}, u32[]{:S(2)}) copy-start(f32[32,1024]{1,0:T(8,128)} %param.27) | copy-start | bytes 393220
  468.1 27.6 %copy-start.17 = (f32[128,1024]{1,0:T(8,128)S(1)}, f32[128,1024]{1,0:T(8,128)}, u32[]{:S(2)}) copy-start(f32[128,1024]{1,0:T(8,128)} %param.28) | copy-start | bytes 1572868
  468.1 28.5 %copy-start.18 = (f32[128,1024]{1,0:T(8,128)S(1)}, f32[128,1024]{1,0:T(8,128)}, u32[]{:S(2)}) copy-start(f32[128,1024]{1,0:T(8,128)} %param.29) | copy-start | bytes 1572868
  (2 other events, 2.1 us)
